TPU v7x, 512 devices: a whole 4x4x16 slice. The times are simulated.
512 devices in a mesh: dp: 8 (over x, core), ctx: 64 (over y, z).
Axes of the slice: x: 4, y: 4, z: 16, core: 2. Of those that a mesh axis runs over, the one named last changes fastest.
Arguments:
- peak_rows: bfloat16 [8, 16384, 1024], P('dp', 'ctx'), may hold values from -6 to 6
- row_route: int32 [8, 16384], P('dp', 'ctx'), may hold values from -1 to 7, as said below
- inducing: bfloat16 [256, 1024], replicated, may hold values from -320 to 320
- w_key: bfloat16 [1024, 1024], P('ctx'), may hold values from -0.1875 to 0.1875
- w_value: bfloat16 [1024, 1024], P('ctx'), may hold values from -0.1875 to 0.1875
- w_query: bfloat16 [1024, 1024], P('ctx'), may hold values from -0.1875 to 0.1875
Outputs:
- summary: bfloat16 [8, 256, 1024], P('dp')
- local_queries: bfloat16 [8, 16384, 1024], P('dp', 'ctx')
- moved_queries: bfloat16 [8, 8192, 1024], P('dp', 'ctx')
Inputs may be any that keep to these rules, and one draw needn't show every extreme that they name: `row_route`: in each set the live rows (route 0 or more) are its first rows and the rest are -1; every set has 256 or more live rows and one set has all 16384. A live row's route is its own set's index or another set's index. Among the 256 rows of one device at most 144 keep their own set's index and at most 16 name any one other set; a device whose rows are all live keeps exactly 144 and names every other set exactly 16 times.
All inputs are finite; a program needn't handle non-finite values.
Results may differ from a plain program's by a relative error of at most 0.00705.
The roundings to bfloat16 on the way count: a program that leaves them out, or rounds other values in their place, can miss the bound.
Values may be sent and summed in bfloat16 or wider, within the bound.
A program may use at most 64 MiB of HBM per device.

v0:
```python
import math

import jax
import jax.numpy as jnp
from jax import lax
from jax.sharding import PartitionSpec as P

HEADS = 8


masked_low = -1e30


def project(rows_in, full_key, full_value, full_query):
    keys = jnp.dot(rows_in, full_key, preferred_element_type=jnp.float32).astype(jnp.bfloat16)
    values = jnp.dot(rows_in, full_value, preferred_element_type=jnp.float32).astype(jnp.bfloat16)
    queries = jnp.dot(rows_in, full_query, preferred_element_type=jnp.float32).astype(jnp.bfloat16)
    return (keys, values, queries)


def partials(inducing, keys, values, live):
    point_count, width = inducing.shape
    head_size = width // HEADS
    row_count = keys.shape[0]
    query_heads = inducing.reshape(point_count, HEADS, head_size)
    key_heads = keys.reshape(row_count, HEADS, head_size)
    value_heads = values.reshape(row_count, HEADS, head_size)
    scores = jnp.einsum(
        "mhe,nhe->hmn", query_heads, key_heads, preferred_element_type=jnp.float32
    ) / math.sqrt(head_size)
    scores = jnp.where(live[None, None, :], scores, jnp.float32(masked_low))
    top_score = jnp.max(scores, axis=2)
    exp_terms = jnp.where(
        live[None, None, :], jnp.exp(scores - top_score[:, :, None]), jnp.float32(0.0)
    )
    totals = jnp.sum(exp_terms, axis=2)
    probs = exp_terms.astype(jnp.bfloat16)
    weighted = jnp.einsum("hmn,nhe->hme", probs, value_heads, preferred_element_type=jnp.float32)
    return (top_score, totals, weighted)


def local(peak_rows, row_route, inducing, w_key, w_value, w_query):
    rows_in = peak_rows[0]
    route_row = row_route[0]
    rows_n, width = rows_in.shape
    capacity = rows_n // 16
    groups = lax.axis_size("dp")
    own_group = lax.axis_index("dp")
    full_key, full_value, full_query = (
        lax.all_gather(w_key, "ctx", axis=0, tiled=True),
        lax.all_gather(w_value, "ctx", axis=0, tiled=True),
        lax.all_gather(w_query, "ctx", axis=0, tiled=True),
    )
    row_ids = jnp.arange(rows_n, dtype=jnp.int32)
    targets = jnp.arange(groups, dtype=jnp.int32)
    outgoing = (route_row[:, None] == targets[None, :]) & (targets[None, :] != own_group)
    send_slot = jnp.cumsum(outgoing.astype(jnp.int32), axis=0) - 1
    flat_slot = jnp.where(outgoing, targets[None, :] * capacity + send_slot, groups * capacity)
    row_grid = jnp.broadcast_to(row_ids[:, None], (rows_n, groups))
    send_table = (
        jnp.full((groups * capacity,), rows_n, jnp.int32)
        .at[flat_slot.reshape(-1)]
        .set(row_grid.reshape(-1), mode="drop")
    )
    keep_mask = route_row == own_group
    all_keys, all_values, row_queries = project(rows_in, full_key, full_value, full_query)
    all_live = route_row >= 0
    local_queries = jnp.where(keep_mask[:, None], row_queries, jnp.zeros_like(row_queries))
    padded_queries = jnp.concatenate([row_queries, jnp.zeros((1, width), jnp.bfloat16)], axis=0)
    sent_queries = jnp.take(padded_queries, send_table, axis=0).reshape(groups, capacity, width)
    moved_queries = lax.all_to_all(sent_queries, "dp", split_axis=0, concat_axis=0, tiled=True)
    top_score, totals, weighted = partials(inducing, all_keys, all_values, all_live)
    point_count = inducing.shape[0]
    common_top = lax.pmax(top_score, "ctx")
    rescale = jnp.exp(top_score - common_top)
    totals, weighted = lax.psum((totals * rescale, weighted * rescale[:, :, None]), "ctx")
    summary = (
        (weighted / totals[:, :, None])
        .transpose(1, 0, 2)
        .reshape(point_count, width)
        .astype(jnp.bfloat16)
    )
    return (summary[None], local_queries[None], moved_queries.reshape(1, groups * capacity, width))


def solution(mesh):
    placed = (
        P("dp", "ctx", None),
        P("dp", "ctx"),
        P(),
        P("ctx", None),
        P("ctx", None),
        P("ctx", None),
    )
    return jax.shard_map(
        local,
        mesh=mesh,
        in_specs=placed,
        out_specs=(P("dp", None, None), P("dp", "ctx", None), P("dp", "ctx", None)),
        check_vma=False,
    )
```

profile of v0, /device:TPU:6, one launch (start us, length us, event | category | flops | bytes accessed | tf_op | source)
XLA Modules:
  0.0 718.9 jit_solution(15896566487452774125)
XLA Ops:
  7.2 0.7 all-gather.4.cloned.1.call-update
  8.0 0.7 all-gather.6.cloned.1.call-update
  8.7 0.7 all-gather.8.cloned.1.call-update
  9.5 0.8 fusion.26
  10.2 0.6 reduce-window.6
  10.8 0.2 slice_reduce_fusion
  11.1 0.8 bitcast_select_fusion
  11.8 0.1 copy.18
  11.9 0.1 reshape.127
  12.1 0.1 reshape.142
  12.2 8.0 %scatter_custom_fusion = s32[128]{0:T(128)S(1)} fusion(s32[2048]{0:T(1024)S(1)} %bitcast.66, s32[2048]{0:T(1024)S(1)} %reshape.142, s32[]{:T(128)} %constant.22.clone.1), kind=kCustom, calls=%fused_computation.52 | custom fusion | bytes 516 | tf_op jit(solution)/shard_map/scatter | solution.py:63
  20.3 0.1 broadcast_in_dim.83
  20.4 0.7 broadcast_compare_fusion
  21.0 135.3 %all-gather.4.cloned.1.call-done = bf16[1024,1024]{1,0:T(8,128)(2,1)} async-done(((bf16[16,1024]{1,0:T(8,128)(2,1)}), bf16[1024,1024]{1,0:T(8,128)(2,1)}) %all-gather.4.cloned.1.call-update) | async-done | bytes 2097168 | tf_op jit(solution)/shard_map/all_gather | solution.py:50
  156.4 2.3 fusion.4
  158.7 0.5 bitcast_reduce_fusion
  159.2 144.2 %pmax.7 = f32[8,256]{1,0:T(8,128)S(1)} all-reduce(f32[8,256]{1,0:T(8,128)S(1)} %get-tuple-element.10), channel_id=1, replica_groups=mesh['dp'=8,'ctx'=64] {'ctx'}, use_global_device_ids=true, to_apply=%region_1.2 | all-reduce | flops 2048 | bytes 16384 | tf_op jit(solution)/shard_map/pmax | solution.py:74
  303.4 0.6 fusion.2
  304.1 2.3 fusion.5
  306.4 2.0 convolution_multiply_fusion
  308.4 127.8 %all-gather.8.cloned.1.call-done = bf16[1024,1024]{1,0:T(8,128)(2,1)} async-done(((bf16[16,1024]{1,0:T(8,128)(2,1)}), bf16[1024,1024]{1,0:T(8,128)(2,1)}) %all-gather.8.cloned.1.call-update) | async-done | bytes 2097168 | tf_op jit(solution)/shard_map/all_gather | solution.py:52
  436.2 2.3 convolution_convert_fusion
  438.6 0.9 gather_fusion
  439.4 0.8 broadcast_select_fusion
  440.2 4.8 all-to-all-start
  445.0 143.9 %psum.15 = f32[8,256]{1,0:T(8,128)S(1)} all-reduce(f32[8,256]{1,0:T(8,128)S(1)} %get-tuple-element.6), channel_id=1, replica_groups=mesh['dp'=8,'ctx'=64] {'ctx'}, use_global_device_ids=true, to_apply=%region_4.5 | all-reduce | flops 2048 | bytes 16384 | tf_op jit(solution)/shard_map/psum | solution.py:76
  588.9 0.9 select_bitcast_fusion
  589.8 119.1 %all-reduce.3.cloned.1.call-done = f32[8,256,128]{2,1,0:T(8,128)} async-done(((f32[8,256,128]{2,1,0:T(8,128)}), f32[8,256,128]{2,1,0:T(8,128)}) %all-reduce.3.cloned.1.call-update) | async-done | bytes 1048592 | tf_op jit(solution)/shard_map/psum | solution.py:76
  708.9 1.6 fusion.23
  710.5 0.2 copy.17
  710.7 1.0 copy.19
  711.7 0.7 copy.42
  (22 shorter events, 0.3 us)
Async XLA Ops:
  7.2 149.2 %copy-start = (bf16[1,256,1024]{2,1,0:T(8,128)(2,1)S(1)}, bf16[1,256,1024]{2,1,0:T(8,128)(2,1)}, u32[]{:S(2)}) copy-start(bf16[1,256,1024]{2,1,0:T(8,128)(2,1)} %param.6) | copy-start | bytes 1572868
  7.2 149.2 %all-gather.4.cloned.1.call-start = ((), (), s32[]{:S(2)}) async-start(), calls=%async_computation.1 | async-start | bytes 2129920 | tf_op jit(solution)/shard_map/all_gather | solution.py:50
  7.9 150.8 %copy-start.1 = (bf16[256,1024]{1,0:T(8,128)(2,1)S(1)}, bf16[256,1024]{1,0:T(8,128)(2,1)}, u32[]{:S(2)}) copy-start(bf16[256,1024]{1,0:T(8,128)(2,1)} %param.8) | copy-start | bytes 1572868
  7.9 296.1 %all-gather.6.cloned.1.call-start = ((), (), s32[]{:S(2)}) async-start(), calls=%async_computation.2 | async-start | bytes 2129920 | tf_op jit(solution)/shard_map/all_gather | solution.py:51
  8.7 427.5 %all-gather.8.cloned.1.call-start = ((), (), s32[]{:S(2)}) async-start(), calls=%async_computation.4 | async-start | bytes 2129920 | tf_op jit(solution)/shard_map/all_gather | solution.py:52
  9.4 699.5 %all-reduce.3.cloned.1.call-start = ((), (), s32[]{:S(2)}) async-start(), calls=%async_computation.3 | async-start | bytes 2097152 | tf_op jit(solution)/shard_map/psum | solution.py:76
  440.2 149.6 %all-to-all-start = ((bf16[8,16,1024]{2,1,0:T(8,128)(2,1)}), bf16[8,16,1024]{2,1,0:T(8,128)(2,1)S(1)}, u32[]{:S(2)}, u32[]{:S(2)}) async-start(bf16[8,16,1024]{2,1,0:T(8,128)(2,1)} %broadcast_select_fusion), calls=%async_computation | async-start | bytes 524288 | tf_op jit(solution)/shard_map/all_to_all | solution.py:71
Sparse Core Ops, SparseCore 0:
  11.0 145.3 all-gather.3
  159.3 137.0 all-gather.5
  299.4 136.7 all-gather.7
  439.4 269.4 all-reduce.2
where the time goes:
time: 719 us
  waiting for transfers between devices  384 us (53%)
  blocking collectives  288 us (40%)
  between operations  14 us (2%)
  local copies, waits for them, and re-layouts  11.5 us (2%)
  matrix products  9.4 us (1%)
    pmax x1, blocking collectives, local(): common_top = lax.pmax(top_score, 'ctx')  144 us
    psum x1, blocking collectives, local(): lax.psum((totals * rescale, weighted * rescale[:, :, None]), 'ctx')  144 us
    all_gather x1, waiting for transfers between devices, local(): lax.all_gather(w_key, 'ctx', axis=0, tiled=True)  135 us
    all_gather x1, waiting for transfers between devices, local(): lax.all_gather(w_query, 'ctx', axis=0, tiled=True)  128 us
    psum x1, waiting for transfers between devices, local(): lax.psum((totals * rescale, weighted * rescale[:, :, None]), 'ctx')  119 us
  transfers between devices with their start and end apart: 5, of which 3 were waited for; matrix products, arithmetic and copies ran while one was open for 3% of the time, Pallas kernels for 0%

commit v1 on v0

v1 whole, which is shorter than its diff:
```python
import math

import jax
import jax.numpy as jnp
from jax import lax
from jax.experimental import pallas as pl
from jax.experimental.pallas import tpu as pltpu
from jax.sharding import PartitionSpec as P

HEADS = 8
NY = 4
NZ = 16
HALF = NZ // 2
SCORE_FLOOR = -1e30
MESH = pl.DeviceIdType.MESH
VMEM = pl.BlockSpec(memory_space=pltpu.VMEM)


def place():
    dp = lax.axis_index("dp")
    ctx = lax.axis_index("ctx")
    return dp, lax.div(ctx, NZ), lax.rem(ctx, NZ)


def wrap(value, size):
    return lax.rem(value + size, size)


def remote(src, dst, send_sem, recv_sem, dp, y, z):
    return pltpu.make_async_remote_copy(
        src_ref=src,
        dst_ref=dst,
        send_sem=send_sem,
        recv_sem=recv_sem,
        device_id=(dp, y * NZ + z),
        device_id_type=MESH,
    )


def greet(partners):
    barrier = pltpu.get_barrier_semaphore()
    for dp, y, z in partners:
        pl.semaphore_signal(barrier, inc=1, device_id=(dp, y * NZ + z), device_id_type=MESH)
    pl.semaphore_wait(barrier, len(partners))


def gather_kernel(
    wk, wv, wq, kv, qf,
    local_sem, zas, zar, zqs, zqr, ys, yr, fs, fr, qs, qr, pas, par, pqs, pqr,
):
    dp, y, z = place()
    core = lax.rem(dp, 2)
    partner = dp + 1 - 2 * core
    width = wk.shape[1] // 2
    cols = pl.ds(pl.multiple_of(core * width, width), width)
    other = pl.ds(pl.multiple_of((1 - core) * width, width), width)

    def shifted(step, way):
        return wrap(z - step if way == 0 else z + step, NZ)

    def kv_ring(step, way, arriving):
        block = kv.at[:, y, shifted(step + 1 if arriving else step, way), :, cols]
        target = wrap(z + 1 if way == 0 else z - 1, NZ)
        return remote(block, block, zas.at[way, step], zar.at[way, step], dp, y, target)

    def q_ring(step, way, arriving):
        block = qf.at[:, shifted(step + 1 if arriving else step, way), :, cols]
        target = wrap(z + 1 if way == 0 else z - 1, NZ)
        return remote(block, block, zqs.at[way, step], zqr.at[way, step], dp, y, target)

    def kv_side(step, way, side, arriving):
        row = y if not arriving else wrap(y - 1 if side == 0 else y + 1, NY)
        block = kv.at[:, row, shifted(step, way), :, cols]
        slot = 2 * step + way
        target = wrap(y + 1 if side == 0 else y - 1, NY)
        return remote(block, block, ys.at[side, slot], yr.at[side, slot], dp, target, z)

    def kv_pass(step, way, side, arriving):
        hops = 2 if arriving else 1
        row = wrap(y - hops if side == 0 else y + hops, NY)
        block = kv.at[side, row, shifted(step, way), :, cols]
        slot = 2 * step + way
        target = wrap(y + 1 if side == 0 else y - 1, NY)
        return remote(block, block, fs.at[side, slot], fr.at[side, slot], dp, target, z)

    def kv_swap(step, way, arriving):
        block = kv.at[:, :, shifted(step, way), :, other if arriving else cols]
        slot = 2 * step + way
        return remote(block, block, pas.at[slot], par.at[slot], partner, y, z)

    def q_swap(step, way, arriving):
        block = qf.at[:, shifted(step, way), :, other if arriving else cols]
        slot = 2 * step + way
        return remote(block, block, pqs.at[slot], pqr.at[slot], partner, y, z)

    def q_side(hop, arriving):
        row = wrap(y - hop, NY) if arriving else y
        block = qf.at[row, z, :, cols]
        return remote(block, block, qs.at[hop - 1], qr.at[hop - 1], dp, wrap(y + hop, NY), z)

    def stage_kv(step, ways, onward):
        for way in ways:
            if not (isinstance(step, int) and step == 0):
                kv_ring(step - 1, way, True).wait_recv()
        for way in onward:
            kv_ring(step, way, False).start()
        for way in ways:
            for side in (0, 1):
                kv_side(step, way, side, False).start()

    def stage_q(step, ways, onward):
        for way in ways:
            if not (isinstance(step, int) and step == 0):
                q_ring(step - 1, way, True).wait_recv()
        for way in onward:
            q_ring(step, way, False).start()
        for way in ways:
            q_swap(step, way, False).start()

    def stage_pass(step, ways):
        for way in ways:
            for side in (0, 1):
                kv_side(step, way, side, True).wait_recv()
                kv_pass(step, way, side, False).start()

    def stage_swap(step, ways):
        for way in ways:
            for side in (0, 1):
                kv_pass(step, way, side, True).wait_recv()
            kv_swap(step, way, False).start()

    own = [
        pltpu.make_async_copy(wk.at[:, cols], kv.at[0, y, z, :, cols], local_sem.at[0]),
        pltpu.make_async_copy(wv.at[:, cols], kv.at[1, y, z, :, cols], local_sem.at[1]),
        pltpu.make_async_copy(wq.at[:, cols], qf.at[y, z, :, cols], local_sem.at[2]),
    ]
    for copy in own:
        copy.start()
    greet(
        [
            (dp, y, wrap(z + 1, NZ)),
            (dp, y, wrap(z - 1, NZ)),
            (dp, wrap(y + 1, NY), z),
            (dp, wrap(y + 2, NY), z),
            (dp, wrap(y + 3, NY), z),
            (partner, y, z),
        ]
    )
    for copy in own:
        copy.wait()

    both = (0, 1)
    for hop in (1, 3, 2):
        q_side(hop, False).start()
    stage_kv(0, (0,), both)
    for hop in (1, 3, 2):
        q_side(hop, True).wait_recv()
    stage_q(0, (0,), both)
    stage_kv(1, both, both)
    stage_q(1, both, both)
    stage_pass(0, (0,))

    def body(step, carry):
        stage_kv(step, both, both)
        stage_q(step, both, both)
        stage_pass(step - 1, both)

        @pl.when(step > 2)
        def _():
            stage_swap(step - 2, both)

        @pl.when(step == 2)
        def _():
            stage_swap(0, (0,))

        return carry

    lax.fori_loop(2, HALF - 1, body, 0)
    last = HALF - 1
    stage_kv(last, both, (0,))
    stage_q(last, both, (0,))
    stage_pass(last - 1, both)
    stage_swap(last - 2, both)
    stage_kv(HALF, (0,), ())
    stage_q(HALF, (0,), ())
    stage_pass(last, both)
    stage_swap(last - 1, both)
    stage_pass(HALF, (0,))
    stage_swap(last, both)
    stage_swap(HALF, (0,))

    for hop in (1, 2, 3):
        q_side(hop, False).wait_send()

    def finish_slot(step, ways):
        for way in ways:
            kv_swap(step, way, True).wait_recv()
            q_swap(step, way, True).wait_recv()
            kv_swap(step, way, False).wait_send()
            q_swap(step, way, False).wait_send()
            for side in (0, 1):
                kv_side(step, way, side, False).wait_send()
                kv_pass(step, way, side, False).wait_send()

    def finish_ring(step, ways):
        for way in ways:
            kv_ring(step, way, False).wait_send()
            q_ring(step, way, False).wait_send()

    finish_slot(0, (0,))
    finish_ring(0, both)

    def finish(step, carry):
        finish_slot(step, both)
        finish_ring(step, both)
        return carry

    lax.fori_loop(1, last, finish, 0)
    finish_slot(last, both)
    finish_ring(last, (0,))
    finish_slot(HALF, (0,))


def gather_weights(w_key, w_value, w_query):
    depth, width = w_key.shape
    dma = pltpu.SemaphoreType.DMA
    slots = 2 * HALF + 1
    kv, qf = pl.pallas_call(
        gather_kernel,
        out_shape=(
            jax.ShapeDtypeStruct((2, NY, NZ, depth, width), w_key.dtype),
            jax.ShapeDtypeStruct((NY, NZ, depth, width), w_key.dtype),
        ),
        in_specs=[VMEM] * 3,
        out_specs=(VMEM, VMEM),
        scratch_shapes=[
            dma((3,)),
            dma((2, HALF)), dma((2, HALF)),
            dma((2, HALF)), dma((2, HALF)),
            dma((2, slots)), dma((2, slots)),
            dma((2, slots)), dma((2, slots)),
            dma((3,)), dma((3,)),
            dma((slots,)), dma((slots,)),
            dma((slots,)), dma((slots,)),
        ],
        compiler_params=pltpu.CompilerParams(collective_id=0, has_side_effects=True),
        name="gather_weights",
    )(w_key, w_value, w_query)
    full = NY * NZ * depth
    return kv.reshape(2, full, width), qf.reshape(full, width)


def attend_kernel(rows, route_col, route_row, inducing, kv, qf, local_out, sent_out, part_out):
    own = lax.axis_index("dp")
    row_count, width = rows.shape
    groups = sent_out.shape[0] // 16
    points = inducing.shape[0]
    head_size = width // HEADS
    scale = jnp.float32(1.0 / math.sqrt(head_size))

    column = route_col[...]
    live = column >= 0
    keep = column == own

    lane_route = jnp.broadcast_to(route_row[...], (groups, row_count))
    target = lax.broadcasted_iota(jnp.int32, (groups, row_count), 0)
    outgoing = jnp.where((lane_route == target) & (target != own), 1.0, 0.0)
    before = lax.broadcasted_iota(jnp.int32, (row_count, row_count), 0)
    after = lax.broadcasted_iota(jnp.int32, (row_count, row_count), 1)
    ramp = jnp.where(before <= after, 1.0, 0.0).astype(jnp.bfloat16)
    rank = jnp.dot(outgoing.astype(jnp.bfloat16), ramp, preferred_element_type=jnp.float32)
    slot = lax.broadcasted_iota(jnp.int32, (16, row_count), 0).astype(jnp.float32) + 1.0
    picks = jnp.concatenate(
        [
            jnp.where(
                (jnp.broadcast_to(rank[g : g + 1], (16, row_count)) == slot)
                & (jnp.broadcast_to(outgoing[g : g + 1], (16, row_count)) > 0.5),
                1.0,
                0.0,
            )
            for g in range(groups)
        ],
        axis=0,
    ).astype(jnp.bfloat16)
    stat_row = lax.broadcasted_iota(jnp.int32, (8, points), 0)

    pair = 2 * head_size
    for block in range(width // pair):
        cols = pl.ds(block * pair, pair)
        keys = jnp.dot(rows[...], kv[0, :, cols], preferred_element_type=jnp.float32)
        keys = keys.astype(jnp.bfloat16)
        values = jnp.dot(rows[...], kv[1, :, cols], preferred_element_type=jnp.float32)
        values = values.astype(jnp.bfloat16)
        queries = jnp.dot(rows[...], qf[:, cols], preferred_element_type=jnp.float32)
        queries = queries.astype(jnp.bfloat16)
        local_out[:, cols] = jnp.where(keep, queries.astype(jnp.float32), 0.0).astype(jnp.bfloat16)
        sent_out[:, cols] = jnp.dot(
            picks, queries, preferred_element_type=jnp.float32
        ).astype(jnp.bfloat16)
        for sub in range(2):
            head = 2 * block + sub
            lanes = slice(sub * head_size, (sub + 1) * head_size)
            scores = lax.dot_general(
                keys[:, lanes],
                inducing[:, pl.ds(head * head_size, head_size)],
                (((1,), (1,)), ((), ())),
                preferred_element_type=jnp.float32,
            )
            scores = jnp.where(live, scores * scale, jnp.float32(SCORE_FLOOR))
            top = jnp.max(scores, axis=0, keepdims=True)
            terms = jnp.where(live, jnp.exp(scores - top), 0.0)
            total = jnp.sum(terms, axis=0, keepdims=True)
            weighted = lax.dot_general(
                values[:, lanes],
                terms.astype(jnp.bfloat16),
                (((0,), (0,)), ((), ())),
                preferred_element_type=jnp.float32,
            )
            part_out[head, 0:head_size, :] = weighted
            part_out[head, head_size : head_size + 8, :] = jnp.where(
                stat_row < 4,
                jnp.broadcast_to(top, (8, points)),
                jnp.broadcast_to(total, (8, points)),
            )


def attend(rows, route, inducing, kv, qf, groups):
    row_count, width = rows.shape
    points = inducing.shape[0]
    head_size = width // HEADS
    return pl.pallas_call(
        attend_kernel,
        out_shape=(
            jax.ShapeDtypeStruct((row_count, width), jnp.bfloat16),
            jax.ShapeDtypeStruct((groups * 16, width), jnp.bfloat16),
            jax.ShapeDtypeStruct((HEADS, head_size + 8, points), jnp.float32),
        ),
        in_specs=[VMEM] * 6,
        out_specs=(VMEM,) * 3,
        name="attend",
    )(rows, route.reshape(row_count, 1), route.reshape(1, row_count), inducing, kv, qf)


ORDER = (8, 7, 9, 6, 10, 5, 11, 4, 12, 3, 13, 2, 14, 1, 15)


def combine_kernel(
    part, sent, summary, moved,
    from_y, to_z, from_z, piece,
    local_sem, ms, mr, ys, yr, zs, zr, gs, gr, hs, hr,
):
    dp, y, z = place()
    groups = sent.shape[0]
    head_size = summary.shape[1]
    quarter = head_size // 4

    greet(
        [(wrap(dp + k, groups), y, z) for k in range(1, groups)]
        + [(dp, wrap(y + k, NY), z) for k in range(1, NY)]
        + [(dp, y, wrap(z + k, NZ)) for k in range(1, NZ)]
    )

    def swap_y(k):
        there = wrap(y + k, NY)
        return remote(
            part.at[pl.ds(2 * there, 2)], from_y.at[k - 1], ys.at[k - 1], yr.at[k - 1], dp, there, z
        )

    for k in (2, 1, 3):
        swap_y(k).start()

    def move(k, arriving):
        there = wrap(dp + k, groups)
        slot = wrap(dp - k, groups) if arriving else dp
        return remote(sent.at[there], moved.at[slot], ms.at[k - 1], mr.at[k - 1], there, y, z)

    for k in range(1, groups):
        move(k, False).start()
    keep_own = pltpu.make_async_copy(sent.at[dp], moved.at[dp], local_sem.at[0])
    keep_own.start()

    for k in range(1, NY):
        swap_y(k).wait_recv()

    stat_row = lax.broadcasted_iota(jnp.int32, (8, 128), 0)
    for head in range(2):
        for half in range(2):
            lanes = slice(half * 128, half * 128 + 128)
            sources = [part.at[2 * y + head]] + [from_y.at[k, head] for k in range(NY - 1)]
            tops = [s[head_size : head_size + 1, lanes] for s in sources]
            totals = [s[head_size + 4 : head_size + 5, lanes] for s in sources]
            top = tops[0]
            for other in tops[1:]:
                top = jnp.maximum(top, other)
            shares = [jnp.exp(t - top) for t in tops]
            total = totals[0] * shares[0]
            for other, share in zip(totals[1:], shares[1:]):
                total = total + other * share
            stats = jnp.where(
                stat_row < 4, jnp.broadcast_to(top, (8, 128)), jnp.broadcast_to(total, (8, 128))
            )
            for group in range(4):
                lines = slice(group * quarter, (group + 1) * quarter)
                value = sources[0][lines, lanes] * shares[0]
                for source, share in zip(sources[1:], shares[1:]):
                    value = value + source[lines, lanes] * share
                slot = head * 8 + half * 4 + group
                to_z[slot, 0:quarter, :] = value
                to_z[slot, quarter : quarter + 8, :] = stats

    def swap_z(k):
        there = wrap(z + k, NZ)
        return remote(
            to_z.at[there], from_z.at[k - 1], zs.at[k - 1], zr.at[k - 1], dp, y, there
        )

    for k in ORDER:
        swap_z(k).start()
    for k in reversed(ORDER):
        swap_z(k).wait_recv()

    sources = [to_z.at[z]] + [from_z.at[k] for k in range(NZ - 1)]
    tops = [s[quarter : quarter + 1, :] for s in sources]
    top = tops[0]
    for other in tops[1:]:
        top = jnp.maximum(top, other)
    value = None
    total = None
    for source, own_top in zip(sources, tops):
        share = jnp.exp(own_top - top)
        term = source[0:quarter, :] * share
        count = source[quarter + 4 : quarter + 5, :] * share
        value = term if value is None else value + term
        total = count if total is None else total + count
    piece[...] = (value / total).astype(jnp.bfloat16)

    def spot(there):
        return summary.at[
            2 * y + lax.div(there, 8),
            pl.ds(pl.multiple_of(lax.rem(there, 4) * quarter, quarter), quarter),
            pl.ds(pl.multiple_of(lax.rem(lax.div(there, 4), 2) * 128, 128), 128),
        ]

    def spread_z(k, arriving):
        owner = wrap(z - k, NZ) if arriving else z
        return remote(
            piece, spot(owner), gs.at[k - 1], gr.at[k - 1], dp, y, wrap(z + k, NZ)
        )

    for k in ORDER:
        spread_z(k, False).start()
    own_piece = pltpu.make_async_copy(piece, spot(z), local_sem.at[1])
    own_piece.start()
    own_piece.wait()
    for k in reversed(ORDER):
        spread_z(k, True).wait_recv()

    def spread_y(k, arriving):
        row = wrap(y - k, NY) if arriving else y
        block = summary.at[pl.ds(2 * row, 2)]
        return remote(block, block, hs.at[k - 1], hr.at[k - 1], dp, wrap(y + k, NY), z)

    for k in (2, 1, 3):
        spread_y(k, False).start()
    for k in range(1, NY):
        spread_y(k, True).wait_recv()
    keep_own.wait()
    for k in range(1, groups):
        move(k, True).wait_recv()
        move(k, False).wait_send()
    for k in range(1, NY):
        swap_y(k).wait_send()
        spread_y(k, False).wait_send()
    for k in range(1, NZ):
        swap_z(k).wait_send()
        spread_z(k, False).wait_send()


def combine(part, sent):
    heads, lines, points = part.shape
    head_size = lines - 8
    groups = sent.shape[0]
    dma = pltpu.SemaphoreType.DMA
    return pl.pallas_call(
        combine_kernel,
        out_shape=(
            jax.ShapeDtypeStruct((heads, head_size, points), jnp.bfloat16),
            jax.ShapeDtypeStruct(sent.shape, sent.dtype),
        ),
        in_specs=[VMEM, VMEM],
        out_specs=(VMEM, VMEM),
        scratch_shapes=[
            pltpu.VMEM((NY - 1, 2, lines, points), jnp.float32),
            pltpu.VMEM((NZ, head_size // 4 + 8, 128), jnp.float32),
            pltpu.VMEM((NZ - 1, head_size // 4 + 8, 128), jnp.float32),
            pltpu.VMEM((head_size // 4, 128), jnp.bfloat16),
            dma((2,)),
            dma((groups - 1,)), dma((groups - 1,)),
            dma((NY - 1,)), dma((NY - 1,)),
            dma((NZ - 1,)), dma((NZ - 1,)),
            dma((NZ - 1,)), dma((NZ - 1,)),
            dma((NY - 1,)), dma((NY - 1,)),
        ],
        compiler_params=pltpu.CompilerParams(collective_id=1, has_side_effects=True),
        name="combine",
    )(part, sent)


def local(peak_rows, row_route, inducing, w_key, w_value, w_query):
    rows = peak_rows[0]
    row_count, width = rows.shape
    groups = lax.axis_size("dp")
    points = inducing.shape[0]
    kv, qf = gather_weights(w_key, w_value, w_query)
    local_queries, sent, part = attend(rows, row_route[0], inducing, kv, qf, groups)
    summary, moved = combine(part, sent.reshape(groups, 16, width))
    summary = summary.transpose(2, 0, 1).reshape(points, width)
    return summary[None], local_queries[None], moved.reshape(1, groups * 16, width)


def solution(mesh):
    placed = (
        P("dp", "ctx", None),
        P("dp", "ctx"),
        P(),
        P("ctx", None),
        P("ctx", None),
        P("ctx", None),
    )
    return jax.shard_map(
        local,
        mesh=mesh,
        in_specs=placed,
        out_specs=(P("dp", None, None), P("dp", "ctx", None), P("dp", "ctx", None)),
        check_vma=False,
    )
```

time: 719 us -> 132 us (0.18)
  waiting for transfers between devices: 384 us -> 0 us
  blocking collectives: 288 us -> 0 us
  Pallas kernels: 0 us -> 124 us
  between operations: 14 us -> 0.65 us
  matrix products: 9.4 us -> 0 us
    all_gather x3 -> x0, waiting for transfers between devices: 263 us -> none  [the longest x1 135 us: local(): lax.all_gather(w_key, 'ctx', axis=0, tiled=True)]
    pmax x1 -> x0, blocking collectives: 144 us -> none  [local(): common_top = lax.pmax(top_score, 'ctx')]
    psum x1 -> x0, blocking collectives: 144 us -> none  [local(): lax.psum((totals * rescale, weighted * rescale[:, :, None]), 'ctx')]
    pallas_call x0 -> x3, Pallas kernels: none -> 124 us  [the longest x1 58.4 us: gather_weights(): pl.pallas_call(gather_kernel, out_shape=(jax.ShapeDtypeStruct((2, NY, NZ,...]
    psum x1 -> x0, waiting for transfers between devices: 119 us -> none  [local(): lax.psum((totals * rescale, weighted * rescale[:, :, None]), 'ctx')]
    dot_general x5 -> x0, matrix products: 9.4 us -> none  [the longest x1 2.3 us: project(): jnp.dot(rows_in, full_value, preferred_element_type=jnp.float32)]
    scatter x1 -> x0, local copies, waits for them, and re-layouts: 8.04 us -> none  [local(): send_table = jnp.full((groups * capacity,), rows_n, jnp.int32).at[flat_sl...]
  transfers between devices with their start and end apart: 5 -> 0, of which waited for: 3 -> 0; matrix products, arithmetic and copies ran while one was open for 3% -> 0% of each run, Pallas kernels for 0% -> 0%
where the time goes in v1:
time: 132 us; the launch traced here: 130 us
  Pallas kernels  124 us (94%)
  local copies, waits for them, and re-layouts  5.19 us (4%)
    pallas_call x1, Pallas kernels, gather_weights(): pl.pallas_call(gather_kernel, out_shape=(jax.ShapeDtypeStruct((2, NY, NZ,...  58.4 us
    pallas_call x1, Pallas kernels, combine(): pl.pallas_call(combine_kernel, out_shape=(jax.ShapeDtypeStruct((heads, he...  56.4 us
    pallas_call x1, Pallas kernels, attend(): pl.pallas_call(attend_kernel, out_shape=(jax.ShapeDtypeStruct((row_count,...  9.57 us
    unnamed x2, local copies, waits for them, and re-layouts  3.71 us

profile of v1, /device:TPU:6, one launch (start us, length us, event | category | flops | bytes accessed | tf_op | source)
XLA Modules:
  0.0 130.3 jit_solution(14012379428775608311)
XLA Ops:
  0.6 1.5 %copy.10.route_col = s32[256,1]{1,0:T(8,128)} copy(s32[256,1]{0,1:T(1,128)} %bitcast.16) | data formatting | bytes 2048 | tf_op jit(solution)/shard_map/reshape;squeeze | solution.py:341
  2.1 58.4 %gather_weights.1 = (bf16[2,4,16,16,1024]{4,3,2,1,0:T(8,128)(2,1)}, bf16[4,16,16,1024]{3,2,1,0:T(8,128)(2,1)}) custom-call(bf16[16,1024]{1,0:T(8,128)(2,1)} %wk.1, bf16[16,1024]{1,0:T(8,128)(2,1)} %wv.1, bf16[16,1024]{1,0:T(8,128)(2,1)} %wq.1), custom_call_target="tpu_custom_call" | custom-call | tf_op jit(solution)/shard_map/gather_weights/pallas_call | solution.py:228
  60.6 9.6 %attend.1 = (bf16[256,1024]{1,0:T(8,128)(2,1)}, bf16[128,1024]{1,0:T(8,128)(2,1)}, f32[8,136,256]{2,1,0:T(8,128)}) custom-call(bf16[256,1024]{1,0:T(8,128)(2,1)} %bitcast.12, s32[256,1]{1,0:T(8,128)} %copy.10.route_col, s32[1,256]{1,0:T(1,128)} %route_row.1, bf16[256,1024]{1,0:T(8,128)(2,1)} %inducing.1, bf16[2,1024,1024]{2,1,0:T(8,128)(2,1)} %bitcast.10, ...), custom_call_target="tpu_custom_call" | custom-call | tf_op jit(solution)/shard_map/attend/pallas_call | solution.py:331
  70.1 56.4 %combine.1 = (bf16[8,128,256]{2,1,0:T(8,128)(2,1)}, bf16[8,16,1024]{2,1,0:T(8,128)(2,1)}) custom-call(f32[8,136,256]{2,1,0:T(8,128)} %get-tuple-element.12.part, bf16[8,16,1024]{2,1,0:T(8,128)(2,1)} %bitcast.15), custom_call_target="tpu_custom_call" | custom-call | tf_op jit(solution)/shard_map/combine/pallas_call | solution.py:484
  126.6 2.0 %copy.11 = bf16[1,256,1024]{2,1,0:T(8,128)(2,1)} copy(bf16[1,256,1024]{1,2,0:T(8,128)(2,1)} %bitcast.13) | data formatting | bytes 1048576
  128.6 1.7 %copy.13 = bf16[1,128,1024]{2,1,0:T(8,128)(2,1)} copy(bf16[1,128,1024]{2,1,0:T(8,128)(2,1)} %bitcast.14) | data formatting | bytes 524288

commit v2 on v0

v2 whole, which is shorter than its diff:
```python
import math

import jax
import jax.numpy as jnp
from jax import lax
from jax.experimental import pallas as pl
from jax.experimental.pallas import tpu as pltpu
from jax.sharding import PartitionSpec as P

HEADS = 8
NY = 4
NZ = 16
HALF = NZ // 2
SCORE_FLOOR = -1e30
MESH = pl.DeviceIdType.MESH
VMEM = pl.BlockSpec(memory_space=pltpu.VMEM)

FAR = (1, NZ - 1)
ORDER = (8, 7, 9, 6, 10, 5, 11, 4, 12, 3, 13, 2, 14, 1, 15)


def place():
    dp = lax.axis_index("dp")
    ctx = lax.axis_index("ctx")
    return dp, lax.div(ctx, NZ), lax.rem(ctx, NZ)


def wrap(value, size):
    return lax.rem(value + size, size)


def remote(src, dst, send_sem, recv_sem, dp, y, z):
    return pltpu.make_async_remote_copy(
        src_ref=src,
        dst_ref=dst,
        send_sem=send_sem,
        recv_sem=recv_sem,
        device_id=(dp, y * NZ + z),
        device_id_type=MESH,
    )


def greet(partners):
    barrier = pltpu.get_barrier_semaphore()
    for dp, y, z in partners:
        pl.semaphore_signal(barrier, inc=1, device_id=(dp, y * NZ + z), device_id_type=MESH)
    pl.semaphore_wait(barrier, len(partners))


def kernel(
    rows, route, inducing, wk, wv, wq,
    summary, local_out, moved,
    kv, qf, sent, own_value, own_stat, out_value, out_stat, in_value, in_stat,
    to_value, to_stat, from_value, from_stat, piece,
    local_sem, zas, zar, zqs, zqr, ys, yr, fs, fr, qs, qr, pas, par, pqs, pqr,
    ms, mr, vs, vr, ss, sr, zvs, zvr, zss, zsr, gs, gr, hs, hr,
):
    dp, y, z = place()
    core = lax.rem(dp, 2)
    partner = dp + 1 - 2 * core
    groups = moved.shape[0]
    row_count, width = rows.shape
    points = inducing.shape[0]
    head_size = width // HEADS
    half_width = width // 2
    quarter = head_size // 4
    cols = pl.ds(pl.multiple_of(core * half_width, half_width), half_width)

    def shifted(step, way):
        return wrap(z - step if way == 0 else z + step, NZ)

    def kv_ring(step, way, arriving):
        block = kv.at[core, shifted(step + 1 if arriving else step, way), y]
        target = wrap(z + 1 if way == 0 else z - 1, NZ)
        return remote(block, block, zas.at[way, step], zar.at[way, step], dp, y, target)

    def q_ring(step, way, arriving):
        block = qf.at[core, shifted(step + 1 if arriving else step, way)]
        target = wrap(z + 1 if way == 0 else z - 1, NZ)
        return remote(block, block, zqs.at[way, step], zqr.at[way, step], dp, y, target)

    def kv_side(step, way, side, arriving):
        row = y if not arriving else wrap(y - 1 if side == 0 else y + 1, NY)
        block = kv.at[core, shifted(step, way), row]
        slot = 2 * step + way
        target = wrap(y + 1 if side == 0 else y - 1, NY)
        return remote(block, block, ys.at[side, slot], yr.at[side, slot], dp, target, z)

    def kv_pass(step, way, side, arriving):
        hops = 2 if arriving else 1
        row = wrap(y - hops if side == 0 else y + hops, NY)
        block = kv.at[core, shifted(step, way), row, side]
        slot = 2 * step + way
        target = wrap(y + 1 if side == 0 else y - 1, NY)
        return remote(block, block, fs.at[side, slot], fr.at[side, slot], dp, target, z)

    def kv_swap(step, way, arriving):
        block = kv.at[1 - core if arriving else core, shifted(step, way)]
        slot = 2 * step + way
        return remote(block, block, pas.at[slot], par.at[slot], partner, y, z)

    def q_swap(step, way, arriving):
        block = qf.at[1 - core if arriving else core, shifted(step, way)]
        slot = 2 * step + way
        return remote(block, block, pqs.at[slot], pqr.at[slot], partner, y, z)

    def q_side(hop, arriving):
        row = wrap(y - hop, NY) if arriving else y
        block = qf.at[core, z, row]
        return remote(block, block, qs.at[hop - 1], qr.at[hop - 1], dp, wrap(y + hop, NY), z)

    def stage_kv(step, ways, onward):
        for way in ways:
            if not (isinstance(step, int) and step == 0):
                kv_ring(step - 1, way, True).wait_recv()
        for way in onward:
            kv_ring(step, way, False).start()
        for way in ways:
            for side in (0, 1):
                kv_side(step, way, side, False).start()

    def stage_q(step, ways, onward):
        for way in ways:
            if not (isinstance(step, int) and step == 0):
                q_ring(step - 1, way, True).wait_recv()
        for way in onward:
            q_ring(step, way, False).start()
        for way in ways:
            q_swap(step, way, False).start()

    def stage_pass(step, ways):
        for way in ways:
            for side in (0, 1):
                kv_side(step, way, side, True).wait_recv()
                kv_pass(step, way, side, False).start()

    def stage_swap(step, ways):
        for way in ways:
            for side in (0, 1):
                kv_pass(step, way, side, True).wait_recv()
            kv_swap(step, way, False).start()

    own = [
        pltpu.make_async_copy(wk.at[:, cols], kv.at[core, z, y, 0], local_sem.at[0]),
        pltpu.make_async_copy(wv.at[:, cols], kv.at[core, z, y, 1], local_sem.at[1]),
        pltpu.make_async_copy(wq.at[:, cols], qf.at[core, z, y], local_sem.at[2]),
    ]
    for copy in own:
        copy.start()
    greet(
        [(wrap(dp + k, groups), y, z) for k in range(1, groups)]
        + [(dp, wrap(y + k, NY), z) for k in range(1, NY)]
        + [(dp, y, wrap(z + k, NZ)) for k in FAR]
    )
    for copy in own:
        copy.wait()

    both = (0, 1)
    for hop in (1, 3, 2):
        q_side(hop, False).start()
    stage_kv(0, (0,), both)
    for hop in (1, 3, 2):
        q_side(hop, True).wait_recv()
    stage_q(0, (0,), both)
    stage_kv(1, both, both)
    stage_q(1, both, both)
    stage_pass(0, (0,))

    def body(step, carry):
        stage_kv(step, both, both)
        stage_q(step, both, both)
        stage_pass(step - 1, both)

        @pl.when(step > 2)
        def _():
            stage_swap(step - 2, both)

        @pl.when(step == 2)
        def _():
            stage_swap(0, (0,))

        return carry

    lax.fori_loop(2, HALF - 1, body, 0)
    last = HALF - 1
    stage_kv(last, both, (0,))
    stage_q(last, both, (0,))
    stage_pass(last - 1, both)
    stage_swap(last - 2, both)
    stage_kv(HALF, (0,), ())
    stage_q(HALF, (0,), ())
    stage_pass(last, both)
    stage_swap(last - 1, both)
    stage_pass(HALF, (0,))
    stage_swap(last, both)
    stage_swap(HALF, (0,))


    lane_route = jnp.broadcast_to(route[...], (groups, row_count))
    target = lax.broadcasted_iota(jnp.int32, (groups, row_count), 0)
    outgoing = jnp.where((lane_route == target) & (target != dp), 1.0, 0.0)
    before = lax.broadcasted_iota(jnp.int32, (row_count, row_count), 0)
    after = lax.broadcasted_iota(jnp.int32, (row_count, row_count), 1)
    ramp = jnp.where(before <= after, 1.0, 0.0).astype(jnp.bfloat16)
    rank = jnp.dot(outgoing.astype(jnp.bfloat16), ramp, preferred_element_type=jnp.float32)
    slot = lax.broadcasted_iota(jnp.int32, (16, row_count), 0).astype(jnp.float32) + 1.0
    picks = jnp.concatenate(
        [
            jnp.where(
                (jnp.broadcast_to(rank[g : g + 1], (16, row_count)) == slot)
                & (jnp.broadcast_to(outgoing[g : g + 1], (16, row_count)) > 0.5),
                1.0,
                0.0,
            )
            for g in range(groups)
        ],
        axis=0,
    ).astype(jnp.bfloat16)
    spread_route = jnp.broadcast_to(route[...].astype(jnp.float32), (row_count, row_count))
    column = jnp.sum(jnp.where(before == after, spread_route, 0.0), axis=1, keepdims=True)
    live = column > -0.5
    keep = column == dp.astype(jnp.float32)

    def product(weights):
        total = None
        span = width // NY
        for line in range(NY):
            block = weights(line)
            term = jnp.dot(
                rows[:, line * span : (line + 1) * span],
                block.reshape(span, block.shape[-1]),
                preferred_element_type=jnp.float32,
            )
            total = term if total is None else total + term
        return total.astype(jnp.bfloat16)

    def settle_kv(step, ways):
        for way in ways:
            kv_swap(step, way, True).wait_recv()

    def settle_q(step, ways):
        for way in ways:
            q_swap(step, way, True).wait_recv()

    def settle_kv_body(step, carry):
        settle_kv(step, both)
        return carry

    def settle_q_body(step, carry):
        settle_q(step, both)
        return carry

    settle_kv(0, (0,))
    lax.fori_loop(1, HALF, settle_kv_body, 0)
    settle_kv(HALF, (0,))

    def swap_value(k):
        there = wrap(y + k, NY)
        return remote(
            out_value.at[k - 1], in_value.at[k - 1], vs.at[k - 1], vr.at[k - 1], dp, there, z
        )

    def swap_stat(k):
        there = wrap(y + k, NY)
        return remote(
            out_stat.at[k - 1], in_stat.at[k - 1], ss.at[k - 1], sr.at[k - 1], dp, there, z
        )

    stat_row = lax.broadcasted_iota(jnp.int32, (8, points), 0)
    scale = jnp.float32(1.0 / math.sqrt(head_size))
    pair = 2 * head_size
    for k in (2, 1, 3, 0):
        block = wrap(y + k, NY)
        side = lax.div(block, 2)
        lanes = pl.ds(pl.multiple_of(lax.rem(block, 2) * pair, pair), pair)
        keys = product(lambda line: kv[side, :, line, 0, :, lanes])
        values = product(lambda line: kv[side, :, line, 1, :, lanes])
        for sub in range(2):
            span = slice(sub * head_size, (sub + 1) * head_size)
            offset = pl.multiple_of(block * pair + sub * head_size, head_size)
            scores = lax.dot_general(
                keys[:, span],
                inducing[:, pl.ds(offset, head_size)],
                (((1,), (1,)), ((), ())),
                preferred_element_type=jnp.float32,
            )
            scores = jnp.where(live, scores * scale, jnp.float32(SCORE_FLOOR))
            top = jnp.max(scores, axis=0, keepdims=True)
            terms = jnp.where(live, jnp.exp(scores - top), 0.0)
            total = jnp.sum(terms, axis=0, keepdims=True)
            weighted = lax.dot_general(
                values[:, span],
                terms.astype(jnp.bfloat16),
                (((0,), (0,)), ((), ())),
                preferred_element_type=jnp.float32,
            )
            stats = jnp.where(
                stat_row < 4,
                jnp.broadcast_to(top, (8, points)),
                jnp.broadcast_to(total, (8, points)),
            )
            if k == 0:
                own_value[sub] = weighted
                own_stat[sub] = stats
            else:
                out_value[k - 1, sub] = weighted.astype(jnp.bfloat16)
                out_stat[k - 1, sub] = stats
        if k:
            swap_stat(k).start()
            swap_value(k).start()

    settle_q(0, (0,))
    lax.fori_loop(1, HALF, settle_q_body, 0)
    settle_q(HALF, (0,))
    for block in range(NY):
        lanes = slice((block % 2) * pair, (block % 2 + 1) * pair)
        queries = product(lambda line: qf[block // 2, :, line, :, lanes])
        span = slice(block * pair, (block + 1) * pair)
        local_out[:, span] = jnp.where(keep, queries.astype(jnp.float32), 0.0).astype(jnp.bfloat16)
        chosen = jnp.dot(picks, queries, preferred_element_type=jnp.float32)
        sent[:, :, span] = chosen.astype(jnp.bfloat16).reshape(groups, 16, pair)

    def move(k, arriving):
        there = wrap(dp + k, groups)
        place_at = wrap(dp - k, groups) if arriving else dp
        return remote(sent.at[there], moved.at[place_at], ms.at[k - 1], mr.at[k - 1], there, y, z)

    for k in range(1, groups):
        move(k, False).start()
    keep_own = pltpu.make_async_copy(sent.at[dp], moved.at[dp], local_sem.at[3])
    keep_own.start()

    for k in (2, 1, 3):
        swap_stat(k).wait_recv()
        swap_value(k).wait_recv()

    stat_row = lax.broadcasted_iota(jnp.int32, (8, 128), 0)
    for head in range(2):
        for half in range(2):
            lanes = slice(half * 128, half * 128 + 128)
            values = [own_value.at[head]] + [in_value.at[k, head] for k in range(NY - 1)]
            stats = [own_stat.at[head]] + [in_stat.at[k, head] for k in range(NY - 1)]
            tops = [s[0:1, lanes] for s in stats]
            totals = [s[4:5, lanes] for s in stats]
            top = tops[0]
            for other in tops[1:]:
                top = jnp.maximum(top, other)
            shares = [jnp.exp(t - top) for t in tops]
            total = totals[0] * shares[0]
            for other, share in zip(totals[1:], shares[1:]):
                total = total + other * share
            to_stat[2 * head + half] = jnp.where(
                stat_row < 4, jnp.broadcast_to(top, (8, 128)), jnp.broadcast_to(total, (8, 128))
            )
            for group in range(4):
                lines = slice(group * quarter, (group + 1) * quarter)
                value = values[0][lines, lanes] * shares[0]
                for source, share in zip(values[1:], shares[1:]):
                    value = value + source[lines, lanes].astype(jnp.float32) * share
                to_value[head * 8 + half * 4 + group] = value.astype(jnp.bfloat16)

    def part_stat(k):
        there = wrap(z + k, NZ)
        return remote(
            to_stat.at[lax.div(there, 4)], from_stat.at[k - 1], zss.at[k - 1], zsr.at[k - 1],
            dp, y, there,
        )

    def part_value(k):
        there = wrap(z + k, NZ)
        return remote(
            to_value.at[there], from_value.at[k - 1], zvs.at[k - 1], zvr.at[k - 1], dp, y, there
        )

    for k in ORDER:
        part_stat(k).start()
        part_value(k).start()
    for k in reversed(ORDER):
        part_stat(k).wait_recv()
        part_value(k).wait_recv()

    values = [to_value.at[z]] + [from_value.at[k] for k in range(NZ - 1)]
    stats = [to_stat.at[lax.div(z, 4)]] + [from_stat.at[k] for k in range(NZ - 1)]
    tops = [s[0:1, :] for s in stats]
    top = tops[0]
    for other in tops[1:]:
        top = jnp.maximum(top, other)
    value = None
    total = None
    for source, stat, own_top in zip(values, stats, tops):
        share = jnp.exp(own_top - top)
        term = source[...].astype(jnp.float32) * share
        count = stat[4:5, :] * share
        value = term if value is None else value + term
        total = count if total is None else total + count
    piece[...] = (value / total).astype(jnp.bfloat16)

    def spot(row, there):
        return summary.at[
            2 * row + lax.div(there, 8),
            pl.ds(pl.multiple_of(lax.rem(there, 4) * quarter, quarter), quarter),
            pl.ds(pl.multiple_of(lax.rem(lax.div(there, 4), 2) * 128, 128), 128),
        ]

    def spread_z(k, arriving):
        owner = wrap(z - k, NZ) if arriving else z
        return remote(
            piece, spot(y, owner), gs.at[k - 1], gr.at[k - 1], dp, y, wrap(z + k, NZ)
        )

    def spread_y(k, j, arriving):
        block = spot(wrap(y - j, NY) if arriving else y, wrap(z - k, NZ))
        source = piece if k == 0 else block
        return remote(
            source, block, hs.at[j - 1, k], hr.at[j - 1, k], dp, wrap(y + j, NY), z
        )

    for k in ORDER:
        spread_z(k, False).start()
    own_piece = pltpu.make_async_copy(piece, spot(y, z), local_sem.at[4])
    own_piece.start()
    for j in (2, 1, 3):
        spread_y(0, j, False).start()
    for k in reversed(ORDER):
        spread_z(k, True).wait_recv()
        for j in (2, 1, 3):
            spread_y(k, j, False).start()
    own_piece.wait()
    keep_own.wait()
    for k in range(NZ):
        for j in range(1, NY):
            spread_y(k, j, True).wait_recv()
    for k in range(1, groups):
        move(k, True).wait_recv()
        move(k, False).wait_send()
    for k in range(1, NY):
        swap_value(k).wait_send()
        swap_stat(k).wait_send()
    for k in range(1, NZ):
        part_value(k).wait_send()
        part_stat(k).wait_send()
        spread_z(k, False).wait_send()
    for k in range(NZ):
        for j in range(1, NY):
            spread_y(k, j, False).wait_send()

    for hop in (1, 2, 3):
        q_side(hop, False).wait_send()

    def finish_slot(step, ways):
        for way in ways:
            kv_swap(step, way, False).wait_send()
            q_swap(step, way, False).wait_send()
            for side in (0, 1):
                kv_side(step, way, side, False).wait_send()
                kv_pass(step, way, side, False).wait_send()

    def finish_ring(step, ways):
        for way in ways:
            kv_ring(step, way, False).wait_send()
            q_ring(step, way, False).wait_send()

    finish_slot(0, (0,))
    finish_ring(0, both)

    def finish(step, carry):
        finish_slot(step, both)
        finish_ring(step, both)
        return carry

    lax.fori_loop(1, last, finish, 0)
    finish_slot(last, both)
    finish_ring(last, (0,))
    finish_slot(HALF, (0,))


def local(peak_rows, row_route, inducing, w_key, w_value, w_query):
    rows = peak_rows[0]
    row_count, width = rows.shape
    depth = w_key.shape[0]
    groups = lax.axis_size("dp")
    points = inducing.shape[0]
    head_size = width // HEADS
    half = width // 2
    quarter = head_size // 4
    slots = 2 * HALF + 1
    dma = pltpu.SemaphoreType.DMA
    low, wide = jnp.bfloat16, jnp.float32
    summary, local_queries, moved = pl.pallas_call(
        kernel,
        out_shape=(
            jax.ShapeDtypeStruct((HEADS, head_size, points), low),
            jax.ShapeDtypeStruct((row_count, width), low),
            jax.ShapeDtypeStruct((groups, 16, width), low),
        ),
        in_specs=[VMEM] * 6,
        out_specs=(VMEM,) * 3,
        scratch_shapes=[
            pltpu.VMEM((2, NZ, NY, 2, depth, half), low),
            pltpu.VMEM((2, NZ, NY, depth, half), low),
            pltpu.VMEM((groups, 16, width), low),
            pltpu.VMEM((2, head_size, points), wide),
            pltpu.VMEM((2, 8, points), wide),
            pltpu.VMEM((NY - 1, 2, head_size, points), low),
            pltpu.VMEM((NY - 1, 2, 8, points), wide),
            pltpu.VMEM((NY - 1, 2, head_size, points), low),
            pltpu.VMEM((NY - 1, 2, 8, points), wide),
            pltpu.VMEM((NZ, quarter, 128), low),
            pltpu.VMEM((4, 8, 128), wide),
            pltpu.VMEM((NZ - 1, quarter, 128), low),
            pltpu.VMEM((NZ - 1, 8, 128), wide),
            pltpu.VMEM((quarter, 128), low),
            dma((5,)),
            dma((2, HALF)), dma((2, HALF)),
            dma((2, HALF)), dma((2, HALF)),
            dma((2, slots)), dma((2, slots)),
            dma((2, slots)), dma((2, slots)),
            dma((NY - 1,)), dma((NY - 1,)),
            dma((slots,)), dma((slots,)),
            dma((slots,)), dma((slots,)),
            dma((groups - 1,)), dma((groups - 1,)),
            dma((NY - 1,)), dma((NY - 1,)),
            dma((NY - 1,)), dma((NY - 1,)),
            dma((NZ - 1,)), dma((NZ - 1,)),
            dma((NZ - 1,)), dma((NZ - 1,)),
            dma((NZ - 1,)), dma((NZ - 1,)),
            dma((NY - 1, NZ)), dma((NY - 1, NZ)),
        ],
        compiler_params=pltpu.CompilerParams(collective_id=0, has_side_effects=True),
        name="encode",
    )(rows, row_route, inducing, w_key, w_value, w_query)
    summary = summary.transpose(2, 0, 1).reshape(points, width)
    return summary[None], local_queries[None], moved.reshape(1, groups * 16, width)


def solution(mesh):
    placed = (
        P("dp", "ctx", None),
        P("dp", "ctx"),
        P(),
        P("ctx", None),
        P("ctx", None),
        P("ctx", None),
    )
    return jax.shard_map(
        local,
        mesh=mesh,
        in_specs=placed,
        out_specs=(P("dp", None, None), P("dp", "ctx", None), P("dp", "ctx", None)),
        check_vma=False,
    )
```

time: 719 us -> 99.4 us (0.14)
  waiting for transfers between devices: 384 us -> 0 us
  blocking collectives: 288 us -> 0 us
  Pallas kernels: 0 us -> 94.7 us
  between operations: 14 us -> 0.65 us
  matrix products: 9.4 us -> 0 us
  local copies, waits for them, and re-layouts: 11.5 us -> 3.9 us
    all_gather x3 -> x0, waiting for transfers between devices: 263 us -> none  [the longest x1 135 us: local(): lax.all_gather(w_key, 'ctx', axis=0, tiled=True)]
    pmax x1 -> x0, blocking collectives: 144 us -> none  [local(): common_top = lax.pmax(top_score, 'ctx')]
    psum x1 -> x0, blocking collectives: 144 us -> none  [local(): lax.psum((totals * rescale, weighted * rescale[:, :, None]), 'ctx')]
    psum x1 -> x0, waiting for transfers between devices: 119 us -> none  [local(): lax.psum((totals * rescale, weighted * rescale[:, :, None]), 'ctx')]
    pallas_call x0 -> x1, Pallas kernels: none -> 94.7 us  [local(): pl.pallas_call(kernel, out_shape=(jax.ShapeDtypeStruct((HEADS, head_size,...]
    dot_general x5 -> x0, matrix products: 9.4 us -> none  [the longest x1 2.3 us: project(): jnp.dot(rows_in, full_value, preferred_element_type=jnp.float32)]
    scatter x1 -> x0, local copies, waits for them, and re-layouts: 8.04 us -> none  [local(): send_table = jnp.full((groups * capacity,), rows_n, jnp.int32).at[flat_sl...]
  transfers between devices with their start and end apart: 5 -> 0, of which waited for: 3 -> 0; matrix products, arithmetic and copies ran while one was open for 3% -> 0% of each run, Pallas kernels for 0% -> 0%
where the time goes in v2:
time: 99.4 us; the launch traced here: 99.2 us
  Pallas kernels  94.7 us (95%)
  local copies, waits for them, and re-layouts  3.9 us (4%)
    pallas_call x1, Pallas kernels, local(): pl.pallas_call(kernel, out_shape=(jax.ShapeDtypeStruct((HEADS, head_size,...  94.7 us
    unnamed x7, local copies, waits for them, and re-layouts  3.9 us

profile of v2, /device:TPU:6, one launch (start us, length us, event | category | flops | bytes accessed | tf_op | source)
XLA Modules:
  0.0 99.2 jit_solution(7437293325805875779)
XLA Ops:
  0.6 94.7 %encode.1 = (bf16[8,128,256]{2,1,0:T(8,128)(2,1)}, bf16[256,1024]{1,0:T(8,128)(2,1)}, bf16[8,16,1024]{2,1,0:T(8,128)(2,1)}) custom-call(bf16[256,1024]{1,0:T(8,128)(2,1)} %bitcast.8, s32[1,256]{1,0:T(1,128)} %route.1, bf16[256,1024]{1,0:T(8,128)(2,1)} %inducing.1, bf16[16,1024]{1,0:T(8,128)(2,1)} %wk.1, bf16[16,1024]{1,0:T(8,128)(2,1)} %wv.1, ...), custom_call_target="tpu_custom_call" | custom-call | tf_op jit(solution)/shard_map/encode/pallas_call | solution.py:489
  95.3 0.0 copy-start
  95.3 2.1 %copy.9 = bf16[1,256,1024]{2,1,0:T(8,128)(2,1)} copy(bf16[1,256,1024]{1,2,0:T(8,128)(2,1)} %bitcast.7) | data formatting | bytes 1048576
  97.4 0.0 copy-done
  97.4 0.0 copy-start.1
  97.4 0.8 copy.12
  98.2 0.3 copy-done.1
  98.5 0.7 copy.13
Async XLA Ops:
  95.3 2.1 %copy-start = (bf16[256,1024]{1,0:T(8,128)(2,1)S(1)}, bf16[256,1024]{1,0:T(8,128)(2,1)}, u32[]{:S(2)}) copy-start(bf16[256,1024]{1,0:T(8,128)(2,1)} %get-tuple-element.7) | copy-start | bytes 1572868
  97.4 1.1 %copy-start.1 = (bf16[8,16,1024]{2,1,0:T(8,128)(2,1)S(1)}, bf16[8,16,1024]{2,1,0:T(8,128)(2,1)}, u32[]{:S(2)}) copy-start(bf16[8,16,1024]{2,1,0:T(8,128)(2,1)} %get-tuple-element.8) | copy-start | bytes 786436

commit v3 on v2

--- a/solution.py
+++ b/solution.py
@@ -10,12 +10,21 @@
 HEADS = 8
 NY = 4
 NZ = 16
-HALF = NZ // 2
 SCORE_FLOOR = -1e30
 MESH = pl.DeviceIdType.MESH
 VMEM = pl.BlockSpec(memory_space=pltpu.VMEM)
 
-FAR = (1, NZ - 1)
+NX = 4
+HOPS = (
+    (0, 4, None), (0, -4, None),
+    (-4, 4, 0), (4, -4, 1),
+    (0, 1, None), (0, -1, None), (0, 2, None), (0, -2, None),
+    (-4, 1, None), (-4, -1, None), (-4, 2, None),
+    (4, 1, None), (4, -1, None), (4, -2, None),
+    (8, 1, None), (8, -1, None),
+)
+BLOCKS = (0, -1, 1, -4, 4, -2, 2, 8, -5, 3, -3, 5, -6, 6, 7, -7)
+FAR = (1, 2, 4, NZ - 4, NZ - 2, NZ - 1)
 ORDER = (8, 7, 9, 6, 10, 5, 11, 4, 12, 3, 13, 2, 14, 1, 15)
 
 
@@ -52,7 +61,7 @@
     summary, local_out, moved,
     kv, qf, sent, own_value, own_stat, out_value, out_stat, in_value, in_stat,
     to_value, to_stat, from_value, from_stat, piece,
-    local_sem, zas, zar, zqs, zqr, ys, yr, fs, fr, qs, qr, pas, par, pqs, pqr,
+    local_sem, zas, zar, zqs, zqr, ys, yr, fs, fr, pas, par, qys, qyr, qxs, qxr, qfs, qfr, pqs, pqr,
     ms, mr, vs, vr, ss, sr, zvs, zvr, zss, zsr, gs, gr, hs, hr,
 ):
     dp, y, z = place()
@@ -66,84 +75,71 @@
     quarter = head_size // 4
     cols = pl.ds(pl.multiple_of(core * half_width, half_width), half_width)
 
-    def shifted(step, way):
-        return wrap(z - step if way == 0 else z + step, NZ)
-
-    def kv_ring(step, way, arriving):
-        block = kv.at[core, shifted(step + 1 if arriving else step, way), y]
-        target = wrap(z + 1 if way == 0 else z - 1, NZ)
-        return remote(block, block, zas.at[way, step], zar.at[way, step], dp, y, target)
-
-    def q_ring(step, way, arriving):
-        block = qf.at[core, shifted(step + 1 if arriving else step, way)]
-        target = wrap(z + 1 if way == 0 else z - 1, NZ)
-        return remote(block, block, zqs.at[way, step], zqr.at[way, step], dp, y, target)
-
-    def kv_side(step, way, side, arriving):
+    column_x = lax.div(dp, 2)
+    eighth = width // (2 * NX)
+    q_cols = pl.ds(pl.multiple_of(core * half_width + column_x * eighth, eighth), eighth)
+
+    def at_z(offset):
+        return wrap(z + offset, NZ)
+
+    def kv_hop(hop, arriving):
+        block, ahead, part = HOPS[hop]
+        spot = kv.at[core, at_z(block - ahead if arriving else block), y]
+        if part is not None:
+            spot = spot.at[part]
+        return remote(spot, spot, zas.at[hop], zar.at[hop], dp, y, at_z(ahead))
+
+    def q_hop(hop, arriving):
+        block, ahead, _ = HOPS[hop]
+        spot = qf.at[core, column_x, y, at_z(block - ahead if arriving else block)]
+        return remote(spot, spot, zqs.at[hop], zqr.at[hop], dp, y, at_z(ahead))
+
+    def kv_side(block, side, arriving):
         row = y if not arriving else wrap(y - 1 if side == 0 else y + 1, NY)
-        block = kv.at[core, shifted(step, way), row]
-        slot = 2 * step + way
+        spot = kv.at[core, at_z(block), row]
+        slot = BLOCKS.index(block)
         target = wrap(y + 1 if side == 0 else y - 1, NY)
-        return remote(block, block, ys.at[side, slot], yr.at[side, slot], dp, target, z)
-
-    def kv_pass(step, way, side, arriving):
+        return remote(spot, spot, ys.at[side, slot], yr.at[side, slot], dp, target, z)
+
+    def kv_pass(block, side, arriving):
         hops = 2 if arriving else 1
         row = wrap(y - hops if side == 0 else y + hops, NY)
-        block = kv.at[core, shifted(step, way), row, side]
-        slot = 2 * step + way
+        spot = kv.at[core, at_z(block), row, side]
+        slot = BLOCKS.index(block)
         target = wrap(y + 1 if side == 0 else y - 1, NY)
-        return remote(block, block, fs.at[side, slot], fr.at[side, slot], dp, target, z)
-
-    def kv_swap(step, way, arriving):
-        block = kv.at[1 - core if arriving else core, shifted(step, way)]
-        slot = 2 * step + way
-        return remote(block, block, pas.at[slot], par.at[slot], partner, y, z)
-
-    def q_swap(step, way, arriving):
-        block = qf.at[1 - core if arriving else core, shifted(step, way)]
-        slot = 2 * step + way
-        return remote(block, block, pqs.at[slot], pqr.at[slot], partner, y, z)
-
-    def q_side(hop, arriving):
-        row = wrap(y - hop, NY) if arriving else y
-        block = qf.at[core, z, row]
-        return remote(block, block, qs.at[hop - 1], qr.at[hop - 1], dp, wrap(y + hop, NY), z)
-
-    def stage_kv(step, ways, onward):
-        for way in ways:
-            if not (isinstance(step, int) and step == 0):
-                kv_ring(step - 1, way, True).wait_recv()
-        for way in onward:
-            kv_ring(step, way, False).start()
-        for way in ways:
-            for side in (0, 1):
-                kv_side(step, way, side, False).start()
-
-    def stage_q(step, ways, onward):
-        for way in ways:
-            if not (isinstance(step, int) and step == 0):
-                q_ring(step - 1, way, True).wait_recv()
-        for way in onward:
-            q_ring(step, way, False).start()
-        for way in ways:
-            q_swap(step, way, False).start()
-
-    def stage_pass(step, ways):
-        for way in ways:
-            for side in (0, 1):
-                kv_side(step, way, side, True).wait_recv()
-                kv_pass(step, way, side, False).start()
-
-    def stage_swap(step, ways):
-        for way in ways:
-            for side in (0, 1):
-                kv_pass(step, way, side, True).wait_recv()
-            kv_swap(step, way, False).start()
+        return remote(spot, spot, fs.at[side, slot], fr.at[side, slot], dp, target, z)
+
+    def kv_swap(block, arriving):
+        spot = kv.at[1 - core if arriving else core, at_z(block)]
+        slot = BLOCKS.index(block)
+        return remote(spot, spot, pas.at[slot], par.at[slot], partner, y, z)
+
+    def q_side(k, arriving):
+        spot = qf.at[core, column_x, wrap(y - k, NY) if arriving else y]
+        return remote(spot, spot, qys.at[k - 1], qyr.at[k - 1], dp, wrap(y + k, NY), z)
+
+    def q_cross(k, side, arriving):
+        step = 1 if side == 0 else -1
+        source = wrap(column_x - step, NX) if arriving else column_x
+        spot = qf.at[core, source, wrap(y - k, NY)]
+        target = 2 * wrap(column_x + step, NX) + core
+        return remote(spot, spot, qxs.at[side, k], qxr.at[side, k], target, y, z)
+
+    def q_pass(k, arriving):
+        step = 1 if k < 2 else -1
+        source = wrap(column_x - (2 * step if arriving else step), NX)
+        spot = qf.at[core, source, wrap(y - k, NY)]
+        target = 2 * wrap(column_x + step, NX) + core
+        return remote(spot, spot, qfs.at[k], qfr.at[k], target, y, z)
+
+    def q_swap(k, arriving):
+        spot = qf.at[1 - core if arriving else core, wrap(column_x + k, NX)]
+        return remote(spot, spot, pqs.at[k], pqr.at[k], partner, y, z)
 
     own = [
         pltpu.make_async_copy(wk.at[:, cols], kv.at[core, z, y, 0], local_sem.at[0]),
         pltpu.make_async_copy(wv.at[:, cols], kv.at[core, z, y, 1], local_sem.at[1]),
-        pltpu.make_async_copy(wq.at[:, cols], qf.at[core, z, y], local_sem.at[2]),
+        pltpu.make_async_copy(wq.at[:, q_cols], qf.at[core, column_x, y, z], local_sem.at[2]),
     ]
     for copy in own:
         copy.start()
@@ -155,46 +151,97 @@
     for copy in own:
         copy.wait()
 
-    both = (0, 1)
-    for hop in (1, 3, 2):
-        q_side(hop, False).start()
-    stage_kv(0, (0,), both)
-    for hop in (1, 3, 2):
-        q_side(hop, True).wait_recv()
-    stage_q(0, (0,), both)
-    stage_kv(1, both, both)
-    stage_q(1, both, both)
-    stage_pass(0, (0,))
-
-    def body(step, carry):
-        stage_kv(step, both, both)
-        stage_q(step, both, both)
-        stage_pass(step - 1, both)
-
-        @pl.when(step > 2)
-        def _():
-            stage_swap(step - 2, both)
-
-        @pl.when(step == 2)
-        def _():
-            stage_swap(0, (0,))
-
-        return carry
-
-    lax.fori_loop(2, HALF - 1, body, 0)
-    last = HALF - 1
-    stage_kv(last, both, (0,))
-    stage_q(last, both, (0,))
-    stage_pass(last - 1, both)
-    stage_swap(last - 2, both)
-    stage_kv(HALF, (0,), ())
-    stage_q(HALF, (0,), ())
-    stage_pass(last, both)
-    stage_swap(last - 1, both)
-    stage_pass(HALF, (0,))
-    stage_swap(last, both)
-    stage_swap(HALF, (0,))
-
+    def side_out(*blocks):
+        for block in blocks:
+            for side in (0, 1):
+                kv_side(block, side, False).start()
+
+    def pass_on(*blocks):
+        for block in blocks:
+            for side in (0, 1):
+                kv_side(block, side, True).wait_recv()
+                kv_pass(block, side, False).start()
+
+    def swap_out(*blocks):
+        for block in blocks:
+            for side in (0, 1):
+                kv_pass(block, side, True).wait_recv()
+            kv_swap(block, False).start()
+
+    def go(*hops):
+        for hop in hops:
+            kv_hop(hop, False).start()
+
+    def arrive(*hops):
+        for hop in hops:
+            kv_hop(hop, True).wait_recv()
+
+    q_hops = tuple(hop for hop in range(len(HOPS)) if hop != 3)
+
+    def q_go(*hops):
+        for hop in hops:
+            q_hop(hop, False).start()
+
+    def q_arrive(*hops):
+        for hop in hops:
+            q_hop(hop, True).wait_recv()
+
+    go(0, 1, 4, 5, 6, 7)
+    side_out(0)
+    q_go(0, 1, 4, 5, 6, 7)
+    arrive(4, 5)
+    side_out(-1, 1)
+    arrive(0)
+    go(2, 8, 9, 10)
+    arrive(1)
+    go(3, 11, 12, 13)
+    side_out(-4, 4)
+    q_arrive(0, 1)
+    q_go(2, 8, 9, 10, 11, 12, 13)
+    pass_on(0)
+    arrive(6, 7)
+    side_out(-2, 2)
+    pass_on(-1, 1)
+    arrive(2, 3)
+    go(14, 15)
+    side_out(8)
+    q_arrive(2)
+    q_go(14, 15)
+    arrive(8, 9, 11, 12)
+    side_out(-5, 3, -3, 5)
+    arrive(10, 13)
+    side_out(-6, 6)
+    arrive(14, 15)
+    side_out(7, -7)
+    pass_on(-4, 4)
+    swap_out(0)
+    q_arrive(*(hop for hop in q_hops if hop not in (0, 1, 2)))
+    for k in (2, 1, 3):
+        q_side(k, False).start()
+    for side in (0, 1):
+        q_cross(0, side, False).start()
+    pass_on(-2, 2)
+    swap_out(-1, 1)
+    pass_on(8, -5)
+    swap_out(-4, 4)
+    pass_on(3, -3)
+    swap_out(-2, 2)
+    pass_on(5, -6)
+    swap_out(8, -5)
+    for k in (1, 3, 2):
+        q_side(k, True).wait_recv()
+        for side in (0, 1):
+            q_cross(k, side, False).start()
+    pass_on(6, 7, -7)
+    swap_out(3, -3, 5, -6)
+    for k in range(NY):
+        for side in (0, 1):
+            q_cross(k, side, True).wait_recv()
+    for k in range(NY):
+        q_pass(k, False).start()
+    for k in (0, 1, 3):
+        q_swap(k, False).start()
+    swap_out(6, 7, -7)
 
     lane_route = jnp.broadcast_to(route[...], (groups, row_count))
     target = lax.broadcasted_iota(jnp.int32, (groups, row_count), 0)
@@ -234,25 +281,8 @@
             total = term if total is None else total + term
         return total.astype(jnp.bfloat16)
 
-    def settle_kv(step, ways):
-        for way in ways:
-            kv_swap(step, way, True).wait_recv()
-
-    def settle_q(step, ways):
-        for way in ways:
-            q_swap(step, way, True).wait_recv()
-
-    def settle_kv_body(step, carry):
-        settle_kv(step, both)
-        return carry
-
-    def settle_q_body(step, carry):
-        settle_q(step, both)
-        return carry
-
-    settle_kv(0, (0,))
-    lax.fori_loop(1, HALF, settle_kv_body, 0)
-    settle_kv(HALF, (0,))
+    for block in BLOCKS:
+        kv_swap(block, True).wait_recv()
 
     def swap_value(k):
         there = wrap(y + k, NY)
@@ -309,12 +339,22 @@
             swap_stat(k).start()
             swap_value(k).start()
 
-    settle_q(0, (0,))
-    lax.fori_loop(1, HALF, settle_q_body, 0)
-    settle_q(HALF, (0,))
+    for k in range(NY):
+        q_pass(k, True).wait_recv()
+    q_swap(2, False).start()
+    for k in range(NX):
+        q_swap(k, True).wait_recv()
     for block in range(NY):
-        lanes = slice((block % 2) * pair, (block % 2 + 1) * pair)
-        queries = product(lambda line: qf[block // 2, :, line, :, lanes])
+        first = 2 * (block % 2)
+        queries = product(
+            lambda line: jnp.concatenate(
+                [
+                    qf[block // 2, first + e, line].reshape(width // NY, eighth)
+                    for e in range(2)
+                ],
+                axis=1,
+            )
+        )
         span = slice(block * pair, (block + 1) * pair)
         local_out[:, span] = jnp.where(keep, queries.astype(jnp.float32), 0.0).astype(jnp.bfloat16)
         chosen = jnp.dot(picks, queries, preferred_element_type=jnp.float32)
@@ -444,34 +484,22 @@
         for j in range(1, NY):
             spread_y(k, j, False).wait_send()
 
-    for hop in (1, 2, 3):
-        q_side(hop, False).wait_send()
-
-    def finish_slot(step, ways):
-        for way in ways:
-            kv_swap(step, way, False).wait_send()
-            q_swap(step, way, False).wait_send()
-            for side in (0, 1):
-                kv_side(step, way, side, False).wait_send()
-                kv_pass(step, way, side, False).wait_send()
-
-    def finish_ring(step, ways):
-        for way in ways:
-            kv_ring(step, way, False).wait_send()
-            q_ring(step, way, False).wait_send()
-
-    finish_slot(0, (0,))
-    finish_ring(0, both)
-
-    def finish(step, carry):
-        finish_slot(step, both)
-        finish_ring(step, both)
-        return carry
-
-    lax.fori_loop(1, last, finish, 0)
-    finish_slot(last, both)
-    finish_ring(last, (0,))
-    finish_slot(HALF, (0,))
+    for hop in range(len(HOPS)):
+        kv_hop(hop, False).wait_send()
+    for hop in q_hops:
+        q_hop(hop, False).wait_send()
+    for block in BLOCKS:
+        for side in (0, 1):
+            kv_side(block, side, False).wait_send()
+            kv_pass(block, side, False).wait_send()
+        kv_swap(block, False).wait_send()
+    for k in range(1, NY):
+        q_side(k, False).wait_send()
+    for k in range(NY):
+        q_pass(k, False).wait_send()
+        q_swap(k, False).wait_send()
+        for side in (0, 1):
+            q_cross(k, side, False).wait_send()
 
 
 def local(peak_rows, row_route, inducing, w_key, w_value, w_query):
@@ -483,7 +511,6 @@
     head_size = width // HEADS
     half = width // 2
     quarter = head_size // 4
-    slots = 2 * HALF + 1
     dma = pltpu.SemaphoreType.DMA
     low, wide = jnp.bfloat16, jnp.float32
     summary, local_queries, moved = pl.pallas_call(
@@ -497,7 +524,7 @@
         out_specs=(VMEM,) * 3,
         scratch_shapes=[
             pltpu.VMEM((2, NZ, NY, 2, depth, half), low),
-            pltpu.VMEM((2, NZ, NY, depth, half), low),
+            pltpu.VMEM((2, NX, NY, NZ, depth, half // NX), low),
             pltpu.VMEM((groups, 16, width), low),
             pltpu.VMEM((2, head_size, points), wide),
             pltpu.VMEM((2, 8, points), wide),
@@ -511,13 +538,15 @@
             pltpu.VMEM((NZ - 1, 8, 128), wide),
             pltpu.VMEM((quarter, 128), low),
             dma((5,)),
-            dma((2, HALF)), dma((2, HALF)),
-            dma((2, HALF)), dma((2, HALF)),
-            dma((2, slots)), dma((2, slots)),
-            dma((2, slots)), dma((2, slots)),
+            dma((len(HOPS),)), dma((len(HOPS),)),
+            dma((len(HOPS),)), dma((len(HOPS),)),
+            dma((2, NZ)), dma((2, NZ)),
+            dma((2, NZ)), dma((2, NZ)),
+            dma((NZ,)), dma((NZ,)),
             dma((NY - 1,)), dma((NY - 1,)),
-            dma((slots,)), dma((slots,)),
-            dma((slots,)), dma((slots,)),
+            dma((2, NY)), dma((2, NY)),
+            dma((NY,)), dma((NY,)),
+            dma((NX,)), dma((NX,)),
             dma((groups - 1,)), dma((groups - 1,)),
             dma((NY - 1,)), dma((NY - 1,)),
             dma((NY - 1,)), dma((NY - 1,)),

time: 99.4 us -> 95.9 us (0.965); the launches traced: 99.2 us -> 94 us
  Pallas kernels: 94.7 us -> 89.5 us
    pallas_call x1, Pallas kernels: 94.7 us -> 89.5 us  [local(): pl.pallas_call(kernel, out_shape=(jax.ShapeDtypeStruct((HEADS, head_size,...]
where the time goes in v3:
time: 95.9 us; the launch traced here: 94 us
  Pallas kernels  89.5 us (93%)
  local copies, waits for them, and re-layouts  3.9 us (4%)
    pallas_call x1, Pallas kernels, local(): pl.pallas_call(kernel, out_shape=(jax.ShapeDtypeStruct((HEADS, head_size,...  89.5 us
    unnamed x7, local copies, waits for them, and re-layouts  3.9 us

profile of v3, /device:TPU:6, one launch (start us, length us, event | category | flops | bytes accessed | tf_op | source)
XLA Modules:
  0.0 94.0 jit_solution(9569297532158905572)
XLA Ops:
  0.6 89.5 %encode.1 = (bf16[8,128,256]{2,1,0:T(8,128)(2,1)}, bf16[256,1024]{1,0:T(8,128)(2,1)}, bf16[8,16,1024]{2,1,0:T(8,128)(2,1)}) custom-call(bf16[256,1024]{1,0:T(8,128)(2,1)} %bitcast.8, s32[1,256]{1,0:T(1,128)} %route.1, bf16[256,1024]{1,0:T(8,128)(2,1)} %inducing.1, bf16[16,1024]{1,0:T(8,128)(2,1)} %wk.1, bf16[16,1024]{1,0:T(8,128)(2,1)} %wv.1, ...), custom_call_target="tpu_custom_call" | custom-call | tf_op jit(solution)/shard_map/encode/pallas_call | solution.py:516
  90.1 0.0 copy-start
  90.1 2.1 %copy.9 = bf16[1,256,1024]{2,1,0:T(8,128)(2,1)} copy(bf16[1,256,1024]{1,2,0:T(8,128)(2,1)} %bitcast.7) | data formatting | bytes 1048576
  92.2 0.0 copy-done
  92.2 0.0 copy-start.1
  92.2 0.8 copy.12
  93.0 0.3 copy-done.1
  93.3 0.7 copy.13
Async XLA Ops:
  90.1 2.1 %copy-start = (bf16[256,1024]{1,0:T(8,128)(2,1)S(1)}, bf16[256,1024]{1,0:T(8,128)(2,1)}, u32[]{:S(2)}) copy-start(bf16[256,1024]{1,0:T(8,128)(2,1)} %get-tuple-element.7) | copy-start | bytes 1572868
  92.2 1.1 %copy-start.1 = (bf16[8,16,1024]{2,1,0:T(8,128)(2,1)S(1)}, bf16[8,16,1024]{2,1,0:T(8,128)(2,1)}, u32[]{:S(2)}) copy-start(bf16[8,16,1024]{2,1,0:T(8,128)(2,1)} %get-tuple-element.8) | copy-start | bytes 786436

commit v4 on v3

--- a/solution.py
+++ b/solution.py
@@ -59,7 +59,7 @@
 def kernel(
     rows, route, inducing, wk, wv, wq,
     summary, local_out, moved,
-    kv, qf, sent, own_value, own_stat, out_value, out_stat, in_value, in_stat,
+    kv, qf, sent, out_value, out_stat, in_value, in_stat,
     to_value, to_stat, from_value, from_stat, piece,
     local_sem, zas, zar, zqs, zqr, ys, yr, fs, fr, pas, par, qys, qyr, qxs, qxr, qfs, qfr, pqs, pqr,
     ms, mr, vs, vr, ss, sr, zvs, zvr, zss, zsr, gs, gr, hs, hr,
@@ -189,59 +189,6 @@
     go(0, 1, 4, 5, 6, 7)
     side_out(0)
     q_go(0, 1, 4, 5, 6, 7)
-    arrive(4, 5)
-    side_out(-1, 1)
-    arrive(0)
-    go(2, 8, 9, 10)
-    arrive(1)
-    go(3, 11, 12, 13)
-    side_out(-4, 4)
-    q_arrive(0, 1)
-    q_go(2, 8, 9, 10, 11, 12, 13)
-    pass_on(0)
-    arrive(6, 7)
-    side_out(-2, 2)
-    pass_on(-1, 1)
-    arrive(2, 3)
-    go(14, 15)
-    side_out(8)
-    q_arrive(2)
-    q_go(14, 15)
-    arrive(8, 9, 11, 12)
-    side_out(-5, 3, -3, 5)
-    arrive(10, 13)
-    side_out(-6, 6)
-    arrive(14, 15)
-    side_out(7, -7)
-    pass_on(-4, 4)
-    swap_out(0)
-    q_arrive(*(hop for hop in q_hops if hop not in (0, 1, 2)))
-    for k in (2, 1, 3):
-        q_side(k, False).start()
-    for side in (0, 1):
-        q_cross(0, side, False).start()
-    pass_on(-2, 2)
-    swap_out(-1, 1)
-    pass_on(8, -5)
-    swap_out(-4, 4)
-    pass_on(3, -3)
-    swap_out(-2, 2)
-    pass_on(5, -6)
-    swap_out(8, -5)
-    for k in (1, 3, 2):
-        q_side(k, True).wait_recv()
-        for side in (0, 1):
-            q_cross(k, side, False).start()
-    pass_on(6, 7, -7)
-    swap_out(3, -3, 5, -6)
-    for k in range(NY):
-        for side in (0, 1):
-            q_cross(k, side, True).wait_recv()
-    for k in range(NY):
-        q_pass(k, False).start()
-    for k in (0, 1, 3):
-        q_swap(k, False).start()
-    swap_out(6, 7, -7)
 
     lane_route = jnp.broadcast_to(route[...], (groups, row_count))
     target = lax.broadcasted_iota(jnp.int32, (groups, row_count), 0)
@@ -268,6 +215,48 @@
     live = column > -0.5
     keep = column == dp.astype(jnp.float32)
 
+    arrive(4, 5)
+    side_out(-1, 1)
+    arrive(0)
+    go(2, 8, 9, 10)
+    arrive(1)
+    go(3, 11, 12, 13)
+    side_out(-4, 4)
+    pass_on(0)
+    arrive(6, 7)
+    side_out(-2, 2)
+    pass_on(-1, 1)
+    arrive(2, 3)
+    go(14, 15)
+    side_out(8)
+    q_arrive(0, 1)
+    q_go(2, 8, 9, 10, 11, 12, 13)
+    arrive(8, 9, 11, 12)
+    side_out(-5, 3, -3, 5)
+    arrive(10, 13)
+    side_out(-6, 6)
+    pass_on(-4, 4)
+    swap_out(0)
+    arrive(14, 15)
+    side_out(7, -7)
+    q_arrive(2)
+    q_go(14, 15)
+    pass_on(-2, 2)
+    swap_out(-1, 1)
+    pass_on(8, -5)
+    swap_out(-4, 4)
+    pass_on(3, -3)
+    swap_out(-2, 2)
+    pass_on(5, -6)
+    swap_out(8, -5)
+    pass_on(6, 7, -7)
+    q_arrive(*(hop for hop in q_hops if hop not in (0, 1, 2)))
+    for k in (2, 1, 3):
+        q_side(k, False).start()
+    for side in (0, 1):
+        q_cross(0, side, False).start()
+    swap_out(3, -3, 5, -6, 6, 7, -7)
+
     def product(weights):
         total = None
         span = width // NY
@@ -281,28 +270,37 @@
             total = term if total is None else total + term
         return total.astype(jnp.bfloat16)
 
-    for block in BLOCKS:
-        kv_swap(block, True).wait_recv()
-
     def swap_value(k):
         there = wrap(y + k, NY)
-        return remote(
-            out_value.at[k - 1], in_value.at[k - 1], vs.at[k - 1], vr.at[k - 1], dp, there, z
-        )
+        return remote(out_value.at[k], in_value.at[k], vs.at[k], vr.at[k], dp, there, z)
 
     def swap_stat(k):
         there = wrap(y + k, NY)
-        return remote(
-            out_stat.at[k - 1], in_stat.at[k - 1], ss.at[k - 1], sr.at[k - 1], dp, there, z
-        )
-
-    stat_row = lax.broadcasted_iota(jnp.int32, (8, points), 0)
+        return remote(out_stat.at[k], in_stat.at[k], ss.at[k], sr.at[k], dp, there, z)
+
     scale = jnp.float32(1.0 / math.sqrt(head_size))
     pair = 2 * head_size
-    for k in (2, 1, 3, 0):
-        block = wrap(y + k, NY)
-        side = lax.div(block, 2)
-        lanes = pl.ds(pl.multiple_of(lax.rem(block, 2) * pair, pair), pair)
+    for turn in range(NY):
+        side = core if turn < 2 else 1 - core
+        block = 2 * side + turn % 2
+        k = wrap(block - y, NY)
+        lanes = slice((turn % 2) * pair, (turn % 2 + 1) * pair)
+        if turn == 1:
+            for hop in (1, 3, 2):
+                q_side(hop, True).wait_recv()
+                for way in (0, 1):
+                    q_cross(hop, way, False).start()
+        if turn == 2:
+            for piece_of in BLOCKS:
+                kv_swap(piece_of, True).wait_recv()
+        if turn == 3:
+            for hop in range(NY):
+                for way in (0, 1):
+                    q_cross(hop, way, True).wait_recv()
+            for hop in range(NY):
+                q_pass(hop, False).start()
+            for hop in (0, 1, 3):
+                q_swap(hop, False).start()
         keys = product(lambda line: kv[side, :, line, 0, :, lanes])
         values = product(lambda line: kv[side, :, line, 1, :, lanes])
         for sub in range(2):
@@ -324,24 +322,59 @@
                 (((0,), (0,)), ((), ())),
                 preferred_element_type=jnp.float32,
             )
-            stats = jnp.where(
-                stat_row < 4,
-                jnp.broadcast_to(top, (8, points)),
-                jnp.broadcast_to(total, (8, points)),
-            )
-            if k == 0:
-                own_value[sub] = weighted
-                own_stat[sub] = stats
-            else:
-                out_value[k - 1, sub] = weighted.astype(jnp.bfloat16)
-                out_stat[k - 1, sub] = stats
-        if k:
+            out_value[k, sub] = weighted.astype(jnp.bfloat16)
+            out_stat[k, sub] = jnp.concatenate([top, total], axis=0)
+
+        @pl.when(k != 0)
+        def _():
             swap_stat(k).start()
             swap_value(k).start()
 
     for k in range(NY):
         q_pass(k, True).wait_recv()
     q_swap(2, False).start()
+    for k in (2, 1, 3):
+        swap_stat(k).wait_recv()
+        swap_value(k).wait_recv()
+
+    for head in range(2):
+        for half in range(2):
+            lanes = slice(half * 128, half * 128 + 128)
+            values = [out_value.at[0, head]] + [in_value.at[k, head] for k in range(1, NY)]
+            stats = [out_stat.at[0, head]] + [in_stat.at[k, head] for k in range(1, NY)]
+            tops = [s[0:1, lanes] for s in stats]
+            totals = [s[1:2, lanes] for s in stats]
+            top = tops[0]
+            for other in tops[1:]:
+                top = jnp.maximum(top, other)
+            shares = [jnp.exp(t - top) for t in tops]
+            total = totals[0] * shares[0]
+            for other, share in zip(totals[1:], shares[1:]):
+                total = total + other * share
+            to_stat[2 * head + half] = jnp.concatenate([top, total], axis=0)
+            for group in range(4):
+                lines = slice(group * quarter, (group + 1) * quarter)
+                value = values[0][lines, lanes].astype(jnp.float32) * shares[0]
+                for source, share in zip(values[1:], shares[1:]):
+                    value = value + source[lines, lanes].astype(jnp.float32) * share
+                to_value[head * 8 + half * 4 + group] = value.astype(jnp.bfloat16)
+
+    def part_stat(k):
+        there = wrap(z + k, NZ)
+        return remote(
+            to_stat.at[lax.div(there, 4)], from_stat.at[k - 1], zss.at[k - 1], zsr.at[k - 1],
+            dp, y, there,
+        )
+
+    def part_value(k):
+        there = wrap(z + k, NZ)
+        return remote(
+            to_value.at[there], from_value.at[k - 1], zvs.at[k - 1], zvr.at[k - 1], dp, y, there
+        )
+
+    for k in ORDER:
+        part_stat(k).start()
+        part_value(k).start()
     for k in range(NX):
         q_swap(k, True).wait_recv()
     for block in range(NY):
@@ -370,51 +403,6 @@
     keep_own = pltpu.make_async_copy(sent.at[dp], moved.at[dp], local_sem.at[3])
     keep_own.start()
 
-    for k in (2, 1, 3):
-        swap_stat(k).wait_recv()
-        swap_value(k).wait_recv()
-
-    stat_row = lax.broadcasted_iota(jnp.int32, (8, 128), 0)
-    for head in range(2):
-        for half in range(2):
-            lanes = slice(half * 128, half * 128 + 128)
-            values = [own_value.at[head]] + [in_value.at[k, head] for k in range(NY - 1)]
-            stats = [own_stat.at[head]] + [in_stat.at[k, head] for k in range(NY - 1)]
-            tops = [s[0:1, lanes] for s in stats]
-            totals = [s[4:5, lanes] for s in stats]
-            top = tops[0]
-            for other in tops[1:]:
-                top = jnp.maximum(top, other)
-            shares = [jnp.exp(t - top) for t in tops]
-            total = totals[0] * shares[0]
-            for other, share in zip(totals[1:], shares[1:]):
-                total = total + other * share
-            to_stat[2 * head + half] = jnp.where(
-                stat_row < 4, jnp.broadcast_to(top, (8, 128)), jnp.broadcast_to(total, (8, 128))
-            )
-            for group in range(4):
-                lines = slice(group * quarter, (group + 1) * quarter)
-                value = values[0][lines, lanes] * shares[0]
-                for source, share in zip(values[1:], shares[1:]):
-                    value = value + source[lines, lanes].astype(jnp.float32) * share
-                to_value[head * 8 + half * 4 + group] = value.astype(jnp.bfloat16)
-
-    def part_stat(k):
-        there = wrap(z + k, NZ)
-        return remote(
-            to_stat.at[lax.div(there, 4)], from_stat.at[k - 1], zss.at[k - 1], zsr.at[k - 1],
-            dp, y, there,
-        )
-
-    def part_value(k):
-        there = wrap(z + k, NZ)
-        return remote(
-            to_value.at[there], from_value.at[k - 1], zvs.at[k - 1], zvr.at[k - 1], dp, y, there
-        )
-
-    for k in ORDER:
-        part_stat(k).start()
-        part_value(k).start()
     for k in reversed(ORDER):
         part_stat(k).wait_recv()
         part_value(k).wait_recv()
@@ -430,7 +418,7 @@
     for source, stat, own_top in zip(values, stats, tops):
         share = jnp.exp(own_top - top)
         term = source[...].astype(jnp.float32) * share
-        count = stat[4:5, :] * share
+        count = stat[1:2, :] * share
         value = term if value is None else value + term
         total = count if total is None else total + count
     piece[...] = (value / total).astype(jnp.bfloat16)
@@ -526,16 +514,14 @@
             pltpu.VMEM((2, NZ, NY, 2, depth, half), low),
             pltpu.VMEM((2, NX, NY, NZ, depth, half // NX), low),
             pltpu.VMEM((groups, 16, width), low),
-            pltpu.VMEM((2, head_size, points), wide),
-            pltpu.VMEM((2, 8, points), wide),
-            pltpu.VMEM((NY - 1, 2, head_size, points), low),
-            pltpu.VMEM((NY - 1, 2, 8, points), wide),
-            pltpu.VMEM((NY - 1, 2, head_size, points), low),
-            pltpu.VMEM((NY - 1, 2, 8, points), wide),
+            pltpu.VMEM((NY, 2, head_size, points), low),
+            pltpu.VMEM((NY, 2, 2, points), wide),
+            pltpu.VMEM((NY, 2, head_size, points), low),
+            pltpu.VMEM((NY, 2, 2, points), wide),
             pltpu.VMEM((NZ, quarter, 128), low),
-            pltpu.VMEM((4, 8, 128), wide),
+            pltpu.VMEM((4, 2, 128), wide),
             pltpu.VMEM((NZ - 1, quarter, 128), low),
-            pltpu.VMEM((NZ - 1, 8, 128), wide),
+            pltpu.VMEM((NZ - 1, 2, 128), wide),
             pltpu.VMEM((quarter, 128), low),
             dma((5,)),
             dma((len(HOPS),)), dma((len(HOPS),)),
@@ -548,8 +534,8 @@
             dma((NY,)), dma((NY,)),
             dma((NX,)), dma((NX,)),
             dma((groups - 1,)), dma((groups - 1,)),
-            dma((NY - 1,)), dma((NY - 1,)),
-            dma((NY - 1,)), dma((NY - 1,)),
+            dma((NY,)), dma((NY,)),
+            dma((NY,)), dma((NY,)),
             dma((NZ - 1,)), dma((NZ - 1,)),
             dma((NZ - 1,)), dma((NZ - 1,)),
             dma((NZ - 1,)), dma((NZ - 1,)),

time: 95.9 us -> 87 us (0.907); the launches traced: 94 us -> 86.8 us
  Pallas kernels: 89.5 us -> 82.3 us
    pallas_call x1, Pallas kernels: 89.5 us -> 82.3 us  [local(): pl.pallas_call(kernel, out_shape=(jax.ShapeDtypeStruct((HEADS, head_size,...]
where the time goes in v4:
time: 87 us; the launch traced here: 86.8 us
  Pallas kernels  82.3 us (95%)
  local copies, waits for them, and re-layouts  3.9 us (4%)
    pallas_call x1, Pallas kernels, local(): pl.pallas_call(kernel, out_shape=(jax.ShapeDtypeStruct((HEADS, head_size,...  82.3 us
    unnamed x7, local copies, waits for them, and re-layouts  3.9 us

profile of v4, /device:TPU:6, one launch (start us, length us, event | category | flops | bytes accessed | tf_op | source)
XLA Modules:
  0.0 86.8 jit_solution(1481938560240031361)
XLA Ops:
  0.6 82.3 %encode.1 = (bf16[8,128,256]{2,1,0:T(8,128)(2,1)}, bf16[256,1024]{1,0:T(8,128)(2,1)}, bf16[8,16,1024]{2,1,0:T(8,128)(2,1)}) custom-call(bf16[256,1024]{1,0:T(8,128)(2,1)} %bitcast.8, s32[1,256]{1,0:T(1,128)} %route.1, bf16[256,1024]{1,0:T(8,128)(2,1)} %inducing.1, bf16[16,1024]{1,0:T(8,128)(2,1)} %wk.1, bf16[16,1024]{1,0:T(8,128)(2,1)} %wv.1, ...), custom_call_target="tpu_custom_call" | custom-call | tf_op jit(solution)/shard_map/encode/pallas_call | solution.py:504
  82.9 0.0 copy-start
  82.9 2.1 %copy.9 = bf16[1,256,1024]{2,1,0:T(8,128)(2,1)} copy(bf16[1,256,1024]{1,2,0:T(8,128)(2,1)} %bitcast.7) | data formatting | bytes 1048576
  85.0 0.0 copy-done
  85.0 0.0 copy-start.1
  85.0 0.8 copy.12
  85.8 0.3 copy-done.1
  86.1 0.7 copy.13
Async XLA Ops:
  82.9 2.1 %copy-start = (bf16[256,1024]{1,0:T(8,128)(2,1)S(1)}, bf16[256,1024]{1,0:T(8,128)(2,1)}, u32[]{:S(2)}) copy-start(bf16[256,1024]{1,0:T(8,128)(2,1)} %get-tuple-element.7) | copy-start | bytes 1572868
  85.0 1.1 %copy-start.1 = (bf16[8,16,1024]{2,1,0:T(8,128)(2,1)S(1)}, bf16[8,16,1024]{2,1,0:T(8,128)(2,1)}, u32[]{:S(2)}) copy-start(bf16[8,16,1024]{2,1,0:T(8,128)(2,1)} %get-tuple-element.8) | copy-start | bytes 786436

commit v5 on v4

--- a/solution.py
+++ b/solution.py
@@ -61,7 +61,7 @@
     summary, local_out, moved,
     kv, qf, sent, out_value, out_stat, in_value, in_stat,
     to_value, to_stat, from_value, from_stat, piece,
-    local_sem, zas, zar, zqs, zqr, ys, yr, fs, fr, pas, par, qys, qyr, qxs, qxr, qfs, qfr, pqs, pqr,
+    local_sem, zas, zar, zqs, zqr, ys, yr, fs, fr, xs, xr, pas, par, qys, qyr, qxs, qxr, qfs, qfr, pqs, pqr,
     ms, mr, vs, vr, ss, sr, zvs, zvr, zss, zsr, gs, gr, hs, hr,
 ):
     dp, y, z = place()
@@ -82,11 +82,14 @@
     def at_z(offset):
         return wrap(z + offset, NZ)
 
+    mine = lax.rem(column_x, 2)
+    strips = [slice(part * half_width // 2, (part + 1) * half_width // 2) for part in (0, 1)]
+
     def kv_hop(hop, arriving):
         block, ahead, part = HOPS[hop]
-        spot = kv.at[core, at_z(block - ahead if arriving else block), y]
+        spot = kv.at[core, at_z(block - ahead if arriving else block), mine, y]
         if part is not None:
-            spot = spot.at[part]
+            spot = spot.at[:, strips[part]]
         return remote(spot, spot, zas.at[hop], zar.at[hop], dp, y, at_z(ahead))
 
     def q_hop(hop, arriving):
@@ -96,7 +99,7 @@
 
     def kv_side(block, side, arriving):
         row = y if not arriving else wrap(y - 1 if side == 0 else y + 1, NY)
-        spot = kv.at[core, at_z(block), row]
+        spot = kv.at[core, at_z(block), mine, row]
         slot = BLOCKS.index(block)
         target = wrap(y + 1 if side == 0 else y - 1, NY)
         return remote(spot, spot, ys.at[side, slot], yr.at[side, slot], dp, target, z)
@@ -104,15 +107,23 @@
     def kv_pass(block, side, arriving):
         hops = 2 if arriving else 1
         row = wrap(y - hops if side == 0 else y + hops, NY)
-        spot = kv.at[core, at_z(block), row, side]
+        spot = kv.at[core, at_z(block), mine, row, :, strips[side]]
         slot = BLOCKS.index(block)
         target = wrap(y + 1 if side == 0 else y - 1, NY)
         return remote(spot, spot, fs.at[side, slot], fr.at[side, slot], dp, target, z)
 
-    def kv_swap(block, arriving):
-        spot = kv.at[1 - core if arriving else core, at_z(block)]
+    def kv_cross(block, side, arriving):
+        step = 1 if side == 0 else -1
+        spot = kv.at[core, at_z(block), 1 - mine if arriving else mine, :, :, strips[side]]
         slot = BLOCKS.index(block)
-        return remote(spot, spot, pas.at[slot], par.at[slot], partner, y, z)
+        target = 2 * wrap(column_x + step, NX) + core
+        return remote(spot, spot, xs.at[side, slot], xr.at[side, slot], target, y, z)
+
+    def kv_swap(block, turn, arriving):
+        matrix = mine if turn == 0 else 1 - mine
+        spot = kv.at[1 - core if arriving else core, at_z(block), matrix]
+        slot = BLOCKS.index(block)
+        return remote(spot, spot, pas.at[turn, slot], par.at[turn, slot], partner, y, z)
 
     def q_side(k, arriving):
         spot = qf.at[core, column_x, wrap(y - k, NY) if arriving else y]
@@ -136,20 +147,29 @@
         spot = qf.at[1 - core if arriving else core, wrap(column_x + k, NX)]
         return remote(spot, spot, pqs.at[k], pqr.at[k], partner, y, z)
 
-    own = [
-        pltpu.make_async_copy(wk.at[:, cols], kv.at[core, z, y, 0], local_sem.at[0]),
-        pltpu.make_async_copy(wv.at[:, cols], kv.at[core, z, y, 1], local_sem.at[1]),
+    own_key, own_value, own_query = (
+        pltpu.make_async_copy(wk.at[:, cols], kv.at[core, z, 0, y], local_sem.at[0]),
+        pltpu.make_async_copy(wv.at[:, cols], kv.at[core, z, 1, y], local_sem.at[0]),
         pltpu.make_async_copy(wq.at[:, q_cols], qf.at[core, column_x, y, z], local_sem.at[2]),
-    ]
-    for copy in own:
-        copy.start()
+    )
+
+    @pl.when(mine == 0)
+    def _():
+        own_key.start()
+        own_key.wait()
+
+    @pl.when(mine != 0)
+    def _():
+        own_value.start()
+        own_value.wait()
+
+    own_query.start()
     greet(
         [(wrap(dp + k, groups), y, z) for k in range(1, groups)]
         + [(dp, wrap(y + k, NY), z) for k in range(1, NY)]
         + [(dp, y, wrap(z + k, NZ)) for k in FAR]
     )
-    for copy in own:
-        copy.wait()
+    own_query.wait()
 
     def side_out(*blocks):
         for block in blocks:
@@ -166,7 +186,15 @@
         for block in blocks:
             for side in (0, 1):
                 kv_pass(block, side, True).wait_recv()
-            kv_swap(block, False).start()
+            for side in (0, 1):
+                kv_cross(block, side, False).start()
+            kv_swap(block, 0, False).start()
+
+    def settle(*blocks):
+        for block in blocks:
+            for side in (0, 1):
+                kv_cross(block, side, True).wait_recv()
+            kv_swap(block, 1, False).start()
 
     def go(*hops):
         for hop in hops:
@@ -247,15 +275,21 @@
     swap_out(-4, 4)
     pass_on(3, -3)
     swap_out(-2, 2)
+    settle(0, -1, 1)
     pass_on(5, -6)
     swap_out(8, -5)
+    settle(-4, 4)
     pass_on(6, 7, -7)
+    swap_out(3, -3, 5)
+    settle(-2, 2, 8, -5)
+    swap_out(-6, 6, 7, -7)
+    settle(3, -3, 5)
     q_arrive(*(hop for hop in q_hops if hop not in (0, 1, 2)))
     for k in (2, 1, 3):
         q_side(k, False).start()
     for side in (0, 1):
         q_cross(0, side, False).start()
-    swap_out(3, -3, 5, -6, 6, 7, -7)
+    settle(-6, 6, 7, -7)
 
     def product(weights):
         total = None
@@ -292,7 +326,8 @@
                     q_cross(hop, way, False).start()
         if turn == 2:
             for piece_of in BLOCKS:
-                kv_swap(piece_of, True).wait_recv()
+                for part in (0, 1):
+                    kv_swap(piece_of, part, True).wait_recv()
         if turn == 3:
             for hop in range(NY):
                 for way in (0, 1):
@@ -301,8 +336,8 @@
                 q_pass(hop, False).start()
             for hop in (0, 1, 3):
                 q_swap(hop, False).start()
-        keys = product(lambda line: kv[side, :, line, 0, :, lanes])
-        values = product(lambda line: kv[side, :, line, 1, :, lanes])
+        keys = product(lambda line: kv[side, :, 0, line, :, lanes])
+        values = product(lambda line: kv[side, :, 1, line, :, lanes])
         for sub in range(2):
             span = slice(sub * head_size, (sub + 1) * head_size)
             offset = pl.multiple_of(block * pair + sub * head_size, head_size)
@@ -480,7 +515,8 @@
         for side in (0, 1):
             kv_side(block, side, False).wait_send()
             kv_pass(block, side, False).wait_send()
-        kv_swap(block, False).wait_send()
+            kv_cross(block, side, False).wait_send()
+            kv_swap(block, side, False).wait_send()
     for k in range(1, NY):
         q_side(k, False).wait_send()
     for k in range(NY):
@@ -511,7 +547,7 @@
         in_specs=[VMEM] * 6,
         out_specs=(VMEM,) * 3,
         scratch_shapes=[
-            pltpu.VMEM((2, NZ, NY, 2, depth, half), low),
+            pltpu.VMEM((2, NZ, 2, NY, depth, half), low),
             pltpu.VMEM((2, NX, NY, NZ, depth, half // NX), low),
             pltpu.VMEM((groups, 16, width), low),
             pltpu.VMEM((NY, 2, head_size, points), low),
@@ -528,7 +564,8 @@
             dma((len(HOPS),)), dma((len(HOPS),)),
             dma((2, NZ)), dma((2, NZ)),
             dma((2, NZ)), dma((2, NZ)),
-            dma((NZ,)), dma((NZ,)),
+            dma((2, NZ)), dma((2, NZ)),
+            dma((2, NZ)), dma((2, NZ)),
             dma((NY - 1,)), dma((NY - 1,)),
             dma((2, NY)), dma((2, NY)),
             dma((NY,)), dma((NY,)),

time: 87 us -> 90.6 us (1.041); the launches traced: 86.8 us -> 89.1 us
  Pallas kernels: 82.3 us -> 84.5 us
    pallas_call x1, Pallas kernels: 82.3 us -> 84.5 us  [local(): pl.pallas_call(kernel, out_shape=(jax.ShapeDtypeStruct((HEADS, head_size,...]
where the time goes in v5:
time: 90.6 us; the launch traced here: 89.1 us
  Pallas kernels  84.5 us (93%)
  local copies, waits for them, and re-layouts  3.9 us (4%)
    pallas_call x1, Pallas kernels, local(): pl.pallas_call(kernel, out_shape=(jax.ShapeDtypeStruct((HEADS, head_size,...  84.5 us
    unnamed x7, local copies, waits for them, and re-layouts  3.9 us

profile of v5, /device:TPU:6, one launch (start us, length us, event | category | flops | bytes accessed | tf_op | source)
XLA Modules:
  0.0 89.1 jit_solution(6481534049407161037)
XLA Ops:
  0.6 84.5 %encode.1 = (bf16[8,128,256]{2,1,0:T(8,128)(2,1)}, bf16[256,1024]{1,0:T(8,128)(2,1)}, bf16[8,16,1024]{2,1,0:T(8,128)(2,1)}) custom-call(bf16[256,1024]{1,0:T(8,128)(2,1)} %bitcast.8, s32[1,256]{1,0:T(1,128)} %route.1, bf16[256,1024]{1,0:T(8,128)(2,1)} %inducing.1, bf16[16,1024]{1,0:T(8,128)(2,1)} %wk.1, bf16[16,1024]{1,0:T(8,128)(2,1)} %wv.1, ...), custom_call_target="tpu_custom_call" | custom-call | tf_op jit(solution)/shard_map/encode/pallas_call | solution.py:540
  85.2 0.0 copy-start
  85.2 2.1 %copy.9 = bf16[1,256,1024]{2,1,0:T(8,128)(2,1)} copy(bf16[1,256,1024]{1,2,0:T(8,128)(2,1)} %bitcast.7) | data formatting | bytes 1048576
  87.3 0.0 copy-done
  87.3 0.0 copy-start.1
  87.3 0.8 copy.12
  88.1 0.3 copy-done.1
  88.4 0.7 copy.13
Async XLA Ops:
  85.2 2.1 %copy-start = (bf16[256,1024]{1,0:T(8,128)(2,1)S(1)}, bf16[256,1024]{1,0:T(8,128)(2,1)}, u32[]{:S(2)}) copy-start(bf16[256,1024]{1,0:T(8,128)(2,1)} %get-tuple-element.7) | copy-start | bytes 1572868
  87.3 1.1 %copy-start.1 = (bf16[8,16,1024]{2,1,0:T(8,128)(2,1)S(1)}, bf16[8,16,1024]{2,1,0:T(8,128)(2,1)}, u32[]{:S(2)}) copy-start(bf16[8,16,1024]{2,1,0:T(8,128)(2,1)} %get-tuple-element.8) | copy-start | bytes 786436

commit v6 on v4

--- a/solution.py
+++ b/solution.py
@@ -24,6 +24,7 @@
     (8, 1, None), (8, -1, None),
 )
 BLOCKS = (0, -1, 1, -4, 4, -2, 2, 8, -5, 3, -3, 5, -6, 6, 7, -7)
+LATE = (-6, 6, 7, -7)
 FAR = (1, 2, 4, NZ - 4, NZ - 2, NZ - 1)
 ORDER = (8, 7, 9, 6, 10, 5, 11, 4, 12, 3, 13, 2, 14, 1, 15)
 
@@ -109,6 +110,12 @@
         target = wrap(y + 1 if side == 0 else y - 1, NY)
         return remote(spot, spot, fs.at[side, slot], fr.at[side, slot], dp, target, z)
 
+    def kv_direct(block, arriving):
+        spot = kv.at[core, at_z(block), wrap(y + 2, NY) if arriving else y]
+        slot = BLOCKS.index(block)
+        target = wrap(y + 2, NY)
+        return remote(spot, spot, fs.at[0, slot], fr.at[0, slot], dp, target, z)
+
     def kv_swap(block, arriving):
         spot = kv.at[1 - core if arriving else core, at_z(block)]
         slot = BLOCKS.index(block)
@@ -155,17 +162,23 @@
         for block in blocks:
             for side in (0, 1):
                 kv_side(block, side, False).start()
+            if block in LATE:
+                kv_direct(block, False).start()
 
     def pass_on(*blocks):
         for block in blocks:
             for side in (0, 1):
                 kv_side(block, side, True).wait_recv()
-                kv_pass(block, side, False).start()
+                if block not in LATE:
+                    kv_pass(block, side, False).start()
 
     def swap_out(*blocks):
         for block in blocks:
-            for side in (0, 1):
-                kv_pass(block, side, True).wait_recv()
+            if block in LATE:
+                kv_direct(block, True).wait_recv()
+            else:
+                for side in (0, 1):
+                    kv_pass(block, side, True).wait_recv()
             kv_swap(block, False).start()
 
     def go(*hops):
@@ -337,28 +350,6 @@
         swap_stat(k).wait_recv()
         swap_value(k).wait_recv()
 
-    for head in range(2):
-        for half in range(2):
-            lanes = slice(half * 128, half * 128 + 128)
-            values = [out_value.at[0, head]] + [in_value.at[k, head] for k in range(1, NY)]
-            stats = [out_stat.at[0, head]] + [in_stat.at[k, head] for k in range(1, NY)]
-            tops = [s[0:1, lanes] for s in stats]
-            totals = [s[1:2, lanes] for s in stats]
-            top = tops[0]
-            for other in tops[1:]:
-                top = jnp.maximum(top, other)
-            shares = [jnp.exp(t - top) for t in tops]
-            total = totals[0] * shares[0]
-            for other, share in zip(totals[1:], shares[1:]):
-                total = total + other * share
-            to_stat[2 * head + half] = jnp.concatenate([top, total], axis=0)
-            for group in range(4):
-                lines = slice(group * quarter, (group + 1) * quarter)
-                value = values[0][lines, lanes].astype(jnp.float32) * shares[0]
-                for source, share in zip(values[1:], shares[1:]):
-                    value = value + source[lines, lanes].astype(jnp.float32) * share
-                to_value[head * 8 + half * 4 + group] = value.astype(jnp.bfloat16)
-
     def part_stat(k):
         there = wrap(z + k, NZ)
         return remote(
@@ -372,9 +363,36 @@
             to_value.at[there], from_value.at[k - 1], zvs.at[k - 1], zvr.at[k - 1], dp, y, there
         )
 
-    for k in ORDER:
-        part_stat(k).start()
-        part_value(k).start()
+    for turn in (2, 1, 3, 0):
+        spot_of = lax.rem(lax.div(z, 4) + turn, 4)
+        head = lax.div(spot_of, 2)
+        lanes = pl.ds(pl.multiple_of(lax.rem(spot_of, 2) * 128, 128), 128)
+        values = [out_value.at[0, head]] + [in_value.at[k, head] for k in range(1, NY)]
+        stats = [out_stat.at[0, head]] + [in_stat.at[k, head] for k in range(1, NY)]
+        tops = [s[0:1, lanes] for s in stats]
+        totals = [s[1:2, lanes] for s in stats]
+        top = tops[0]
+        for other in tops[1:]:
+            top = jnp.maximum(top, other)
+        shares = [jnp.exp(t - top) for t in tops]
+        total = totals[0] * shares[0]
+        for other, share in zip(totals[1:], shares[1:]):
+            total = total + other * share
+        to_stat[spot_of] = jnp.concatenate([top, total], axis=0)
+        for group in range(4):
+            lines = slice(group * quarter, (group + 1) * quarter)
+            value = values[0][lines, lanes].astype(jnp.float32) * shares[0]
+            for source, share in zip(values[1:], shares[1:]):
+                value = value + source[lines, lanes].astype(jnp.float32) * share
+            to_value[spot_of * 4 + group] = value.astype(jnp.bfloat16)
+        for group in range(4):
+            k = wrap(spot_of * 4 + group - z, NZ)
+
+            @pl.when(k != 0)
+            def _(k=k):
+                part_stat(k).start()
+                part_value(k).start()
+
     for k in range(NX):
         q_swap(k, True).wait_recv()
     for block in range(NY):
@@ -479,7 +497,10 @@
     for block in BLOCKS:
         for side in (0, 1):
             kv_side(block, side, False).wait_send()
-            kv_pass(block, side, False).wait_send()
+            if block not in LATE:
+                kv_pass(block, side, False).wait_send()
+        if block in LATE:
+            kv_direct(block, False).wait_send()
         kv_swap(block, False).wait_send()
     for k in range(1, NY):
         q_side(k, False).wait_send()

time: 87 us -> 87.9 us (1.010)
  the two profiles are of different devices: /device:TPU:6 before, /device:TPU:8 now
where the time goes in v6:
time: 87.9 us; the launch traced here: 87.7 us
  Pallas kernels  83.2 us (95%)
  local copies, waits for them, and re-layouts  3.9 us (4%)
    pallas_call x1, Pallas kernels, local(): pl.pallas_call(kernel, out_shape=(jax.ShapeDtypeStruct((HEADS, head_size,...  83.2 us
    unnamed x7, local copies, waits for them, and re-layouts  3.9 us

profile of v6, /device:TPU:8, one launch (start us, length us, event | category | flops | bytes accessed | tf_op | source)
XLA Modules:
  0.0 87.7 jit_solution(1105027646515916136)
XLA Ops:
  0.6 83.2 %encode.1 = (bf16[8,128,256]{2,1,0:T(8,128)(2,1)}, bf16[256,1024]{1,0:T(8,128)(2,1)}, bf16[8,16,1024]{2,1,0:T(8,128)(2,1)}) custom-call(bf16[256,1024]{1,0:T(8,128)(2,1)} %bitcast.8, s32[1,256]{1,0:T(1,128)} %route.1, bf16[256,1024]{1,0:T(8,128)(2,1)} %inducing.1, bf16[16,1024]{1,0:T(8,128)(2,1)} %wk.1, bf16[16,1024]{1,0:T(8,128)(2,1)} %wv.1, ...), custom_call_target="tpu_custom_call" | custom-call | tf_op jit(solution)/shard_map/encode/pallas_call | solution.py:525
  83.8 0.0 copy-start
  83.8 2.1 %copy.9 = bf16[1,256,1024]{2,1,0:T(8,128)(2,1)} copy(bf16[1,256,1024]{1,2,0:T(8,128)(2,1)} %bitcast.7) | data formatting | bytes 1048576
  85.9 0.0 copy-done
  85.9 0.0 copy-start.1
  85.9 0.8 copy.12
  86.7 0.3 copy-done.1
  87.0 0.7 copy.13
Async XLA Ops:
  83.8 2.1 %copy-start = (bf16[256,1024]{1,0:T(8,128)(2,1)S(1)}, bf16[256,1024]{1,0:T(8,128)(2,1)}, u32[]{:S(2)}) copy-start(bf16[256,1024]{1,0:T(8,128)(2,1)} %get-tuple-element.7) | copy-start | bytes 1572868
  85.9 1.1 %copy-start.1 = (bf16[8,16,1024]{2,1,0:T(8,128)(2,1)S(1)}, bf16[8,16,1024]{2,1,0:T(8,128)(2,1)}, u32[]{:S(2)}) copy-start(bf16[8,16,1024]{2,1,0:T(8,128)(2,1)} %get-tuple-element.8) | copy-start | bytes 786436
